TPU v7x, 256 devices: a whole 4x4x8 slice. The times are simulated.
256 devices in a mesh: seq: 32 (over y, x, core), fsdp: 8 (over z).
Axes of the slice: x: 4, y: 4, z: 8, core: 2. Of those that a mesh axis runs over, the one named last changes fastest.
Arguments:
- normed_block_input: bfloat16 [8, 4096, 8192], P('fsdp', 'seq'), may hold values from -6 to 6
- stored_rotated_queries: bfloat16 [8, 4096, 4096], P('fsdp', 'seq'), may hold values from -640 to 640
- stored_rotated_keys: bfloat16 [8, 4096, 512], P('fsdp', 'seq'), may hold values from -4 to 4
- attention_output_gradient: bfloat16 [8, 4096, 4096], P('fsdp', 'seq'), may hold values from -6 to 6
- frozen_value_weight: bfloat16 [8192, 512], P('fsdp'), may hold values from -0.0625 to 0.0625
- adapter_down_weight: bfloat16 [16, 8192], replicated, may hold values from -0.0625 to 0.0625
- adapter_up_weight: bfloat16 [16, 512], replicated, may hold values from -1.5 to 1.5
- packed_document_lengths: int32 [8, 8], P('fsdp'), may hold values from 1 to 1024, 4096 in all within a row
Outputs:
- input_gradient: bfloat16 [8, 4096, 8192], P('fsdp', 'seq')
- rotated_query_gradient: bfloat16 [8, 4096, 4096], P('fsdp', 'seq')
- rotated_key_gradient: bfloat16 [8, 4096, 512], P('fsdp', 'seq')
- adapter_down_gradient: float32 [16, 8192], replicated
- adapter_up_gradient: float32 [16, 512], replicated
Inputs may be any that keep to these rules, and one draw needn't show every extreme that they name: `packed_document_lengths`: row g holds, in order, the lengths of the 8 documents packed into sequence g; they sum to 4096, and in every row the longest has exactly 1024 tokens.
All inputs are finite; a program needn't handle non-finite values.
Results may differ from a plain program's by a relative error of at most 0.0065.
Values may be sent and summed in bfloat16 or wider, within the bound.
A program may use at most 128 MiB of HBM per device.

v0:
```python
import jax
import jax.numpy as jnp
from jax import lax
from jax.sharding import PartitionSpec as P

HEAD_FEATURES = 128
QUERY_HEADS = 32
KEY_VALUE_HEADS = 4


ADAPTER_SCALE = 2.0
NEG_FILL = -1e30


def contract_trailing(left_rows, right_rows):
    return lax.dot_general(
        left_rows, right_rows, (((1,), (1,)), ((), ())), preferred_element_type=jnp.float32
    )


def body(
    normed_block_input,
    stored_rotated_queries,
    stored_rotated_keys,
    attention_output_gradient,
    frozen_value_weight,
    adapter_down_weight,
    adapter_up_weight,
    packed_document_lengths,
):
    token_rows = normed_block_input.shape[1]
    model_features = normed_block_input.shape[2]
    hidden_activations = normed_block_input.reshape(token_rows, model_features)
    seq_count = lax.axis_size("seq")
    fsdp_count = lax.axis_size("fsdp")
    queries_per_group = QUERY_HEADS // KEY_VALUE_HEADS
    key_value_features = KEY_VALUE_HEADS * HEAD_FEATURES
    inverse = HEAD_FEATURES ** (-0.5)
    adapter_projection = contract_trailing(hidden_activations, adapter_down_weight)
    up_widened = adapter_up_weight.astype(jnp.float32)
    adapter_maps = ADAPTER_SCALE * jnp.dot(
        adapter_projection, up_widened, precision=lax.Precision.HIGHEST
    )
    base_value = jnp.dot(
        hidden_activations,
        lax.all_gather(frozen_value_weight, "fsdp", axis=0, tiled=True),
        preferred_element_type=jnp.float32,
    )
    adapter_values = (base_value + adapter_maps).astype(jnp.bfloat16)
    shaped = (token_rows, QUERY_HEADS, HEAD_FEATURES)
    key_broadcast = jnp.repeat(
        stored_rotated_keys.reshape(token_rows, KEY_VALUE_HEADS, HEAD_FEATURES),
        queries_per_group,
        axis=1,
    )
    value_broadcast = jnp.repeat(
        adapter_values.reshape(token_rows, KEY_VALUE_HEADS, HEAD_FEATURES),
        queries_per_group,
        axis=1,
    )
    head_query, head_key, head_value, head_grad = (
        lax.all_to_all(
            stored_rotated_queries.reshape(shaped), "seq", split_axis=1, concat_axis=0, tiled=True
        ),
        lax.all_to_all(key_broadcast, "seq", split_axis=1, concat_axis=0, tiled=True),
        lax.all_to_all(value_broadcast, "seq", split_axis=1, concat_axis=0, tiled=True),
        lax.all_to_all(
            attention_output_gradient.reshape(shaped),
            "seq",
            split_axis=1,
            concat_axis=0,
            tiled=True,
        ),
    )
    seq_len = head_query.shape[0]
    local_heads = head_query.shape[1]
    block_rows = min(512, seq_len)
    key_reach = block_rows + seq_len // 4
    bounds = jnp.cumsum(packed_document_lengths[0])
    places = jnp.arange(seq_len, dtype=jnp.int32)
    segments = jnp.sum((places[:, None] >= bounds[None, :]).astype(jnp.int32), axis=1)
    grad_keys = jnp.zeros((seq_len, local_heads, HEAD_FEATURES), jnp.float32)
    grad_values = jnp.zeros((seq_len, local_heads, HEAD_FEATURES), jnp.float32)
    query_parts = []
    for block_index in range(seq_len // block_rows):
        first_row = block_index * block_rows
        finish = first_row + block_rows
        opening = max(0, finish - key_reach)
        query_block = head_query[first_row:finish]
        grad_block = head_grad[first_row:finish]
        key_block = head_key[opening:finish]
        value_block = head_value[opening:finish]
        scores = (
            jnp.einsum("qhd,khd->hqk", query_block, key_block, preferred_element_type=jnp.float32)
            * inverse
        )
        allowed = (places[opening:finish][None, :] <= places[first_row:finish][:, None]) & (
            segments[opening:finish][None, :] == segments[first_row:finish][:, None]
        )
        scores = jnp.where(allowed[None], scores, NEG_FILL)
        row_peak = jnp.max(scores, axis=2, keepdims=True)
        weights = jnp.exp(scores - row_peak)
        probs_full = weights / jnp.sum(weights, axis=2, keepdims=True)
        probs_low = probs_full.astype(jnp.bfloat16)
        grad_probs = jnp.einsum(
            "qhd,khd->hqk", grad_block, value_block, preferred_element_type=jnp.float32
        )
        row_delta = jnp.sum(probs_full * grad_probs, axis=2, keepdims=True)
        grad_scores = (probs_full * (grad_probs - row_delta)).astype(jnp.bfloat16)
        query_parts.append(
            jnp.einsum("hqk,khd->qhd", grad_scores, key_block, preferred_element_type=jnp.float32)
            * inverse
        )
        key_part = (
            jnp.einsum("hqk,qhd->khd", grad_scores, query_block, preferred_element_type=jnp.float32)
            * inverse
        )
        value_part = jnp.einsum(
            "hqk,qhd->khd", probs_low, grad_block, preferred_element_type=jnp.float32
        )
        grad_keys = lax.dynamic_update_slice_in_dim(
            grad_keys, grad_keys[opening:finish] + key_part, opening, 0
        )
        grad_values = lax.dynamic_update_slice_in_dim(
            grad_values, grad_values[opening:finish] + value_part, opening, 0
        )
    grad_queries = jnp.concatenate(query_parts, axis=0).astype(jnp.bfloat16)
    token_query = lax.all_to_all(grad_queries, "seq", split_axis=0, concat_axis=1, tiled=True)
    rotated_query_gradient = token_query.reshape(1, token_rows, QUERY_HEADS * HEAD_FEATURES)
    token_key_matrix, token_value_matrix = (
        lax.all_to_all(grad_keys, "seq", split_axis=0, concat_axis=1, tiled=True),
        lax.all_to_all(grad_values, "seq", split_axis=0, concat_axis=1, tiled=True),
    )
    per_key_value_head = token_key_matrix.shape[1] // KEY_VALUE_HEADS
    rotated_key_gradient = (
        token_key_matrix.reshape(token_rows, KEY_VALUE_HEADS, per_key_value_head, HEAD_FEATURES)
        .sum(axis=2)
        .reshape(1, token_rows, key_value_features)
        .astype(jnp.bfloat16)
    )
    value_gradient_matrix = (
        token_value_matrix.reshape(token_rows, KEY_VALUE_HEADS, per_key_value_head, HEAD_FEATURES)
        .sum(axis=2)
        .reshape(token_rows, key_value_features)
    )
    value_grad_low = value_gradient_matrix.astype(jnp.bfloat16)
    adapter_rank_gradient = ADAPTER_SCALE * lax.dot_general(
        value_gradient_matrix, up_widened, (((1,), (1,)), ((), ())), precision=lax.Precision.HIGHEST
    )
    reduced_rank_gradient = adapter_rank_gradient.astype(jnp.bfloat16)
    frozen_path_gradient = contract_trailing(
        value_grad_low, lax.all_gather(frozen_value_weight, "fsdp", axis=0, tiled=True)
    )
    input_gradient = (
        frozen_path_gradient
        + jnp.dot(reduced_rank_gradient, adapter_down_weight, preferred_element_type=jnp.float32)
    ).astype(jnp.bfloat16)
    overall_token_count = token_rows * seq_count * fsdp_count
    down_shard = (
        lax.dot_general(
            reduced_rank_gradient,
            hidden_activations,
            (((0,), (0,)), ((), ())),
            preferred_element_type=jnp.float32,
        )
        / overall_token_count
    )
    up_shard = (
        ADAPTER_SCALE
        * jnp.dot(adapter_projection.T, value_gradient_matrix, precision=lax.Precision.HIGHEST)
        / overall_token_count
    )
    adapter_down_gradient, adapter_up_gradient = lax.psum((down_shard, up_shard), ("seq", "fsdp"))
    return (
        input_gradient.reshape(1, token_rows, model_features),
        rotated_query_gradient,
        rotated_key_gradient,
        adapter_down_gradient,
        adapter_up_gradient,
    )


def solution(mesh):
    placed = (
        P("fsdp", "seq", None),
        P("fsdp", "seq", None),
        P("fsdp", "seq", None),
        P("fsdp", "seq", None),
        P("fsdp", None),
        P(),
        P(),
        P("fsdp", None),
    )
    return jax.shard_map(
        body,
        mesh=mesh,
        in_specs=placed,
        out_specs=(
            P("fsdp", "seq", None),
            P("fsdp", "seq", None),
            P("fsdp", "seq", None),
            P(),
            P(),
        ),
        check_vma=False,
    )
```

profile of v0, /device:TPU:1, one launch (start us, length us, event | category | flops | bytes accessed | tf_op | source)
XLA Modules:
  0.0 525.4 jit_solution(7725692542050299921)
XLA Ops:
  11.0 8.6 %all-to-all-start.2 = ((bf16[128,32,128]{0,2,1:T(8,128)(2,1)}), bf16[128,32,128]{0,2,1:T(8,128)(2,1)S(1)}, u32[]{:S(2)}, u32[]{:S(2)}) async-start(bf16[128,32,128]{0,2,1:T(8,128)(2,1)} %bitcast.418), calls=%async_computation.2 | async-start | bytes 2097152 | tf_op jit(solution)/shard_map/all_to_all | solution.py:67
  21.4 15.2 %all-to-all-done.2 = bf16[128,32,128]{0,2,1:T(8,128)(2,1)S(1)} async-done(((bf16[128,32,128]{0,2,1:T(8,128)(2,1)}), bf16[128,32,128]{0,2,1:T(8,128)(2,1)S(1)}, u32[]{:S(2)}, u32[]{:S(2)}) %all-to-all-start.2) | async-done | bytes 1048608 | tf_op jit(solution)/shard_map/all_to_all | solution.py:67
  38.0 4.1 all-to-all-start.1
  50.0 9.3 %all-to-all-done.1 = bf16[128,32,128]{2,0,1:T(8,128)(2,1)S(1)} async-done(((bf16[128,32,128]{2,0,1:T(8,128)(2,1)}), bf16[128,32,128]{2,0,1:T(8,128)(2,1)S(1)}, u32[]{:S(2)}, u32[]{:S(2)}) %all-to-all-start.1) | async-done | bytes 1048608 | tf_op jit(solution)/shard_map/all_to_all | solution.py:65
  59.3 5.2 all-to-all-start
  71.5 9.7 %all-to-all-done = bf16[128,32,128]{0,2,1:T(8,128)(2,1)} async-done(((bf16[128,32,128]{0,2,1:T(8,128)(2,1)}), bf16[128,32,128]{0,2,1:T(8,128)(2,1)}, u32[]{:S(2)}, u32[]{:S(2)}) %all-to-all-start) | async-done | bytes 1048608 | tf_op jit(solution)/shard_map/all_to_all | solution.py:62
  123.9 3.1 fusion.39
  127.0 3.1 fusion.41
  130.1 3.1 fusion.43
  133.3 3.1 fusion.45
  136.4 4.7 fusion.56
  142.6 4.0 all-to-all-start.4
  146.7 4.1 fusion.47
  150.8 3.1 fusion.49
  153.9 9.9 %all-to-all-done.4 = bf16[128,32,128]{2,0,1:T(8,128)(2,1)S(1)} async-done(((bf16[128,32,128]{2,0,1:T(8,128)(2,1)}), bf16[128,32,128]{2,0,1:T(8,128)(2,1)S(1)}, u32[]{:S(2)}, u32[]{:S(2)}) %all-to-all-start.4) | async-done | bytes 1048608 | tf_op jit(solution)/shard_map/all_to_all | solution.py:66
  163.8 4.7 all-to-all-start.3
  187.9 2.7 multiply_convert_fusion.5
  191.9 2.7 multiply_convert_fusion.4
  206.3 2.7 reduce.48
  214.4 2.6 fusion.37
  217.1 2.6 fusion.35
  219.7 7.8 %all-to-all-start.5 = ((bf16[32,2,8192]{2,1,0:T(2,128)(2,1)}), bf16[32,2,8192]{2,1,0:T(2,128)(2,1)S(1)}, u32[]{:S(2)}, u32[]{:S(2)}) async-start(bf16[32,2,8192]{2,1,0:T(2,128)(2,1)} %reshape.801), calls=%async_computation.5 | async-start | bytes 2097152 | tf_op jit(solution)/shard_map/all_to_all | solution.py:128
  227.6 3.3 fusion.33
  230.9 2.8 fusion.31
  233.7 2.7 fusion.29
  236.4 2.6 fusion.27
  239.0 5.5 %all-to-all-done.5 = bf16[32,2,8192]{2,1,0:T(2,128)(2,1)S(1)} async-done(((bf16[32,2,8192]{2,1,0:T(2,128)(2,1)}), bf16[32,2,8192]{2,1,0:T(2,128)(2,1)S(1)}, u32[]{:S(2)}, u32[]{:S(2)}) %all-to-all-start.5) | async-done | bytes 1048608 | tf_op jit(solution)/shard_map/all_to_all | solution.py:128
  244.5 4.8 all-to-all-start.6
  254.7 92.4 %psum.15 = f32[16,512]{1,0:T(8,128)} all-reduce(f32[16,512]{1,0:T(8,128)S(1)} %convolution_multiply_fusion.25), channel_id=1, replica_groups=mesh['seq'=32,'fsdp'=8] {'seq','fsdp'}, use_global_device_ids=true, to_apply=%region_29.30 | all-reduce | flops 8192 | bytes 65536 | tf_op jit(solution)/shard_map/psum | solution.py:173
  347.1 6.3 %fusion.105 = f32[128,8192]{1,0:T(8,128)S(1)} fusion(bf16[8192,512]{1,0:T(8,128)(2,1)} %all-gather.2.cloned.1.call-done, f32[128,512]{0,1:T(8,128)S(1)} %bitcast.414), kind=kOutput, calls=%fused_computation.176 | convolution fusion | flops 1073807360 | bytes 12845056 | tf_op jit(solution)/shard_map/dot_general | solution.py:16
  355.5 3.4 reshape.802
  366.9 148.8 %all-reduce.4.cloned.1.call-done = f32[16,8192]{1,0:T(8,128)} async-done(((f32[16,8192]{1,0:T(8,128)}), f32[16,8192]{1,0:T(8,128)}) %all-reduce.4.cloned.1.call-update) | async-done | bytes 524304 | tf_op jit(solution)/shard_map/psum | solution.py:173
  (390 shorter events, 118.9 us)
Async XLA Ops:
  8.0 58.4 %copy-start = (bf16[1,128,8192]{2,1,0:T(8,128)(2,1)S(1)}, bf16[1,128,8192]{2,1,0:T(8,128)(2,1)}, u32[]{:S(2)}) copy-start(bf16[1,128,8192]{2,1,0:T(8,128)(2,1)} %param.8) | copy-start | bytes 6291460
  8.0 11.6 %copy-start.59 = (bf16[1,128,512]{2,1,0:T(8,128)(2,1)S(1)}, bf16[1,128,512]{2,1,0:T(8,128)(2,1)}, u32[]{:S(2)}) copy-start(bf16[1,128,512]{2,1,0:T(8,128)(2,1)} %param.10) | copy-start | bytes 393220
  8.0 128.3 %all-gather.2.cloned.1.call-start = ((), (), s32[]{:S(2)}) async-start(), calls=%async_computation.7 | async-start | bytes 9437184 | tf_op jit(solution)/shard_map/all_gather | solution.py:152
  11.0 25.6 %all-to-all-start.2 = ((bf16[128,32,128]{0,2,1:T(8,128)(2,1)}), bf16[128,32,128]{0,2,1:T(8,128)(2,1)S(1)}, u32[]{:S(2)}, u32[]{:S(2)}) async-start(bf16[128,32,128]{0,2,1:T(8,128)(2,1)} %bitcast.418), calls=%async_computation.2 | async-start | bytes 2097152 | tf_op jit(solution)/shard_map/all_to_all | solution.py:67
  19.6 25.3 %copy-start.135 = (s32[1,8]{1,0:T(1,128)S(1)}, s32[1,8]{1,0:T(1,128)}, u32[]{:S(2)}) copy-start(s32[1,8]{1,0:T(1,128)} %param.15) | copy-start | bytes 100
  38.0 28.4 %copy-start.34 = (bf16[16,8192]{1,0:T(8,128)(2,1)S(1)}, bf16[16,8192]{1,0:T(8,128)(2,1)}, u32[]{:S(2)}) copy-start(bf16[16,8192]{1,0:T(8,128)(2,1)} %param.13) | copy-start | bytes 786436
  38.0 21.3 %all-to-all-start.1 = ((bf16[128,32,128]{2,0,1:T(8,128)(2,1)}), bf16[128,32,128]{2,0,1:T(8,128)(2,1)S(1)}, u32[]{:S(2)}, u32[]{:S(2)}) async-start(bf16[128,32,128]{2,0,1:T(8,128)(2,1)} %bitcast.417), calls=%async_computation.1 | async-start | bytes 2097152 | tf_op jit(solution)/shard_map/all_to_all | solution.py:65
  49.9 19.9 %copy-start.44 = (s32[4096]{0:T(1024)}, s32[4096]{0:T(1024)S(1)}, u32[]{:S(2)}) copy-start(s32[4096]{0:T(1024)S(1)} %convert_reduce_fusion) | copy-start | bytes 49156
  59.3 21.9 %all-to-all-start = ((bf16[128,32,128]{0,2,1:T(8,128)(2,1)}), bf16[128,32,128]{0,2,1:T(8,128)(2,1)}, u32[]{:S(2)}, u32[]{:S(2)}) async-start(bf16[128,32,128]{0,2,1:T(8,128)(2,1)} %bitcast.416), calls=%async_computation | async-start | bytes 2097152 | tf_op jit(solution)/shard_map/all_to_all | solution.py:62
  69.8 33.9 %copy-start.126 = (s32[512]{0:T(512)S(1)}, s32[512]{0:T(512)}, u32[]{:S(2)}) copy-start(s32[512]{0:T(512)} %get-tuple-element.55) | copy-start | bytes 6148
  69.8 33.9 %copy-start.127 = (s32[512]{0:T(512)S(1)}, s32[512]{0:T(512)}, u32[]{:S(2)}) copy-start(s32[512]{0:T(512)} %get-tuple-element.94) | copy-start | bytes 6148
  109.1 13.1 %copy-start.14 = (f32[512,1024]{1,0:T(8,128)}, f32[512,1024]{1,0:T(8,128)S(1)}, u32[]{:S(2)}) copy-start(f32[512,1024]{1,0:T(8,128)S(1)} %get-tuple-element.65) | copy-start | bytes 6291460
  110.2 6.6 %copy-start.47 = (bf16[12,128,1,128]{3,1,0,2:T(8,128)(2,1)}, bf16[12,128,1,128]{3,1,0,2:T(8,128)(2,1)S(1)}, u32[]{:S(2)}) copy-start(bf16[12,128,1,128]{3,1,0,2:T(8,128)(2,1)S(1)} %get-tuple-element.27) | copy-start | bytes 1179652
  110.2 9.2 %copy-start.45 = (bf16[12,128,1,128]{3,1,0,2:T(8,128)(2,1)}, bf16[12,128,1,128]{3,1,0,2:T(8,128)(2,1)S(1)}, u32[]{:S(2)}) copy-start(bf16[12,128,1,128]{3,1,0,2:T(8,128)(2,1)S(1)} %get-tuple-element.26) | copy-start | bytes 1179652
  111.3 12.5 %copy-start.12 = (f32[512,1536]{1,0:T(8,128)}, f32[512,1536]{1,0:T(8,128)S(1)}, u32[]{:S(2)}) copy-start(f32[512,1536]{1,0:T(8,128)S(1)} %get-tuple-element.67) | copy-start | bytes 9437188
  111.3 12.5 %copy-start.105 = (f32[512]{0:T(512)}, f32[512]{0:T(512)S(1)}, u32[]{:S(2)}) copy-start(f32[512]{0:T(512)S(1)} %get-tuple-element.66) | copy-start | bytes 6148
  111.9 11.9 %copy-start.116 = (f32[512]{0:T(512)}, f32[512]{0:T(512)S(1)}, u32[]{:S(2)}) copy-start(f32[512]{0:T(512)S(1)} %fusion.9) | copy-start | bytes 6148
  113.0 14.0 %copy-start.10 = (f32[512,1536]{1,0:T(8,128)}, f32[512,1536]{1,0:T(8,128)S(1)}, u32[]{:S(2)}) copy-start(f32[512,1536]{1,0:T(8,128)S(1)} %get-tuple-element.69) | copy-start | bytes 9437188
  113.0 14.0 %copy-start.103 = (f32[512]{0:T(512)}, f32[512]{0:T(512)S(1)}, u32[]{:S(2)}) copy-start(f32[512]{0:T(512)S(1)} %get-tuple-element.68) | copy-start | bytes 6148
  113.6 13.4 %copy-start.114 = (f32[512]{0:T(512)}, f32[512]{0:T(512)S(1)}, u32[]{:S(2)}) copy-start(f32[512]{0:T(512)S(1)} %fusion.11) | copy-start | bytes 6148
  114.6 15.5 %copy-start.5 = (f32[512,1536]{1,0:T(8,128)}, f32[512,1536]{1,0:T(8,128)S(1)}, u32[]{:S(2)}) copy-start(f32[512,1536]{1,0:T(8,128)S(1)} %get-tuple-element.71) | copy-start | bytes 9437188
  114.6 15.5 %copy-start.98 = (f32[512]{0:T(512)}, f32[512]{0:T(512)S(1)}, u32[]{:S(2)}) copy-start(f32[512]{0:T(512)S(1)} %get-tuple-element.70) | copy-start | bytes 6148
  115.2 14.9 %copy-start.110 = (f32[512]{0:T(512)}, f32[512]{0:T(512)S(1)}, u32[]{:S(2)}) copy-start(f32[512]{0:T(512)S(1)} %fusion.13) | copy-start | bytes 6148
  116.3 17.0 %copy-start.3 = (f32[512,1536]{1,0:T(8,128)}, f32[512,1536]{1,0:T(8,128)S(1)}, u32[]{:S(2)}) copy-start(f32[512,1536]{1,0:T(8,128)S(1)} %get-tuple-element.73) | copy-start | bytes 9437188
  116.3 17.0 %copy-start.96 = (f32[512]{0:T(512)}, f32[512]{0:T(512)S(1)}, u32[]{:S(2)}) copy-start(f32[512]{0:T(512)S(1)} %get-tuple-element.72) | copy-start | bytes 6148
  116.9 16.4 %copy-start.108 = (f32[512]{0:T(512)}, f32[512]{0:T(512)S(1)}, u32[]{:S(2)}) copy-start(f32[512]{0:T(512)S(1)} %fusion.15) | copy-start | bytes 6148
  142.6 21.1 %all-to-all-start.4 = ((bf16[128,32,128]{2,0,1:T(8,128)(2,1)}), bf16[128,32,128]{2,0,1:T(8,128)(2,1)S(1)}, u32[]{:S(2)}, u32[]{:S(2)}) async-start(bf16[128,32,128]{2,0,1:T(8,128)(2,1)} %bitcast.419), calls=%async_computation.4 | async-start | bytes 2097152 | tf_op jit(solution)/shard_map/all_to_all | solution.py:66
  163.8 55.9 %all-to-all-start.3 = ((f32[4096,1,128]{2,1,0:T(1,128)}), f32[4096,1,128]{2,1,0:T(1,128)}, u32[]{:S(2)}, u32[]{:S(2)}) async-start(f32[4096,1,128]{2,1,0:T(1,128)} %bitcast.62), calls=%async_computation.3 | async-start | bytes 4194304 | tf_op jit(solution)/shard_map/all_to_all | solution.py:132
  219.7 24.8 %all-to-all-start.5 = ((bf16[32,2,8192]{2,1,0:T(2,128)(2,1)}), bf16[32,2,8192]{2,1,0:T(2,128)(2,1)S(1)}, u32[]{:S(2)}, u32[]{:S(2)}) async-start(bf16[32,2,8192]{2,1,0:T(2,128)(2,1)} %reshape.801), calls=%async_computation.5 | async-start | bytes 2097152 | tf_op jit(solution)/shard_map/all_to_all | solution.py:128
  244.5 8.4 %copy-start.77 = (bf16[16,512]{1,0:T(8,128)(2,1)S(1)}, bf16[16,512]{1,0:T(8,128)(2,1)}, u32[]{:S(2)}) copy-start(bf16[16,512]{1,0:T(8,128)(2,1)} %param.14) | copy-start | bytes 49156
  244.5 119.7 %all-to-all-start.6 = ((f32[4096,1,128]{2,1,0:T(1,128)}), f32[4096,1,128]{2,1,0:T(1,128)}, u32[]{:S(2)}, u32[]{:S(2)}) async-start(f32[4096,1,128]{2,1,0:T(1,128)} %bitcast.139), calls=%async_computation.6 | async-start | bytes 4194304 | tf_op jit(solution)/shard_map/all_to_all | solution.py:131
  249.4 266.3 %all-reduce.4.cloned.1.call-start = ((), (), s32[]{:S(2)}) async-start(), calls=%async_computation.8 | async-start | bytes 1048576 | tf_op jit(solution)/shard_map/psum | solution.py:173
  (114 other events, 279.5 us)
Sparse Core Ops, SparseCore 0:
  10.6 97.6 all-gather.1
Sparse Core Ops, SparseCore 1:
  255.9 259.7 all-reduce.3
where the time goes:
time: 530 us; the launch traced here: 525 us
  waiting for transfers between devices  199 us (38%)
  blocking collectives  92.4 us (17%)
  matrix products  87 us (16%)
  local copies, waits for them, and re-layouts  58.5 us (11%)
  starting transfers between devices  39.3 us (7%)
  other arithmetic  31.5 us (6%)
  between operations  17.6 us (3%)
    psum x1, waiting for transfers between devices, body(): lax.psum((down_shard, up_shard), ('seq', 'fsdp'))  149 us
    psum x1, blocking collectives, body(): lax.psum((down_shard, up_shard), ('seq', 'fsdp'))  92.4 us
    dot_general x8, matrix products, body(): jnp.einsum('hqk,qhd->khd', probs_low, grad_block, preferred_element_type=...  22.6 us
    unnamed x280, local copies, waits for them, and re-layouts  22.2 us
    dot_general x8, matrix products, body(): jnp.einsum('hqk,qhd->khd', grad_scores, query_block, preferred_element_ty...  19.5 us
    all_to_all x1, waiting for transfers between devices, body(): lax.all_to_all(attention_output_gradient.reshape(shaped), 'seq', split_ax...  15.2 us
    slice x9, local copies, waits for them, and re-layouts, body(): query_block = head_query[first_row:finish]  13.6 us
    slice x9, local copies, waits for them, and re-layouts, body(): grad_block = head_grad[first_row:finish]  11.4 us
  transfers between devices with their start and end apart: 9, of which 6 were waited for; matrix products, arithmetic and copies ran while one was open for 31% of the time, Pallas kernels for 0%

commit v1 on v0

--- a/solution.py
+++ b/solution.py
@@ -1,6 +1,10 @@
+import functools
+
 import jax
 import jax.numpy as jnp
 from jax import lax
+from jax.experimental import pallas as pl
+from jax.experimental.pallas import tpu as pltpu
 from jax.sharding import PartitionSpec as P
 
 HEAD_FEATURES = 128
@@ -10,6 +14,205 @@
 
 ADAPTER_SCALE = 2.0
 NEG_FILL = -1e30
+
+
+MESH = pl.DeviceIdType.MESH
+SUM_ROWS = 24
+SUM_LANES = 256
+
+
+def sum_kernel(
+    chips,
+    depth,
+    parts_ref,
+    out_ref,
+    pair_in,
+    pair_total,
+    chip_in,
+    chip_total,
+    depth_in,
+    pair_send,
+    pair_recv,
+    chip_send,
+    chip_recv,
+    depth_send,
+    depth_recv,
+    give_send,
+    give_recv,
+    hand_send,
+    hand_recv,
+):
+    me = lax.axis_index("seq")
+    layer = lax.axis_index("fsdp")
+    chip = me // 2
+    core = lax.rem(me, 2)
+    partner = chip * 2 + 1 - core
+
+    def chip_peer(offset):
+        return lax.rem(chip + offset, chips) * 2 + core
+
+    def depth_peer(offset):
+        return lax.rem(layer + offset, depth)
+
+    barrier = pltpu.get_barrier_semaphore()
+    pl.semaphore_signal(barrier, inc=1, device_id={"seq": partner}, device_id_type=MESH)
+    for offset in range(1, chips):
+        pl.semaphore_signal(
+            barrier, inc=1, device_id={"seq": chip_peer(offset)}, device_id_type=MESH
+        )
+    for offset in range(1, depth):
+        pl.semaphore_signal(
+            barrier, inc=1, device_id={"fsdp": depth_peer(offset)}, device_id_type=MESH
+        )
+    pl.semaphore_wait(barrier, chips + depth - 1)
+
+    pair = pltpu.make_async_remote_copy(
+        src_ref=parts_ref.at[:, 1 - core],
+        dst_ref=pair_in,
+        send_sem=pair_send,
+        recv_sem=pair_recv,
+        device_id={"seq": partner},
+        device_id_type=MESH,
+    )
+    pair.start()
+    pair.wait()
+
+    def add_pair(index, carry):
+        pair_total[index] = parts_ref[index, core] + pair_in[index]
+        return carry
+
+    lax.fori_loop(0, chips, add_pair, 0)
+
+    copies = []
+    for offset in range(1, chips):
+        target = lax.rem(chip + offset, chips)
+        copy = pltpu.make_async_remote_copy(
+            src_ref=pair_total.at[target],
+            dst_ref=chip_in.at[offset - 1],
+            send_sem=chip_send.at[offset - 1],
+            recv_sem=chip_recv.at[offset - 1],
+            device_id={"seq": chip_peer(offset)},
+            device_id_type=MESH,
+        )
+        copy.start()
+        copies.append(copy)
+    for copy in copies:
+        copy.wait()
+    total = pair_total[chip]
+    for offset in range(chips - 1):
+        total = total + chip_in[offset]
+    chip_total[0] = total
+
+    copies = []
+    for offset in range(1, depth):
+        copy = pltpu.make_async_remote_copy(
+            src_ref=chip_total.at[0],
+            dst_ref=depth_in.at[offset - 1],
+            send_sem=depth_send.at[offset - 1],
+            recv_sem=depth_recv.at[offset - 1],
+            device_id={"fsdp": depth_peer(offset)},
+            device_id_type=MESH,
+        )
+        copy.start()
+        copies.append(copy)
+    for copy in copies:
+        copy.wait()
+    rows = [total]
+    for offset in range(depth - 1):
+        rows.append(depth_in[offset])
+    final = rows[0]
+    for row in rows[1:]:
+        final = final + row
+    out_ref[chip, core] = final
+
+    gives = []
+    for offset in range(1, chips):
+        copy = pltpu.make_async_remote_copy(
+            src_ref=out_ref.at[chip, core],
+            dst_ref=out_ref.at[chip, core],
+            send_sem=give_send.at[offset - 1],
+            recv_sem=give_recv.at[offset - 1],
+            device_id={"seq": chip_peer(offset)},
+            device_id_type=MESH,
+        )
+        copy.start()
+        gives.append(copy)
+    hands = []
+    for offset in range(chips):
+        owner = lax.rem(chip + chips - offset, chips)
+        if offset:
+            got = pltpu.make_async_remote_copy(
+                src_ref=out_ref.at[owner, core],
+                dst_ref=out_ref.at[owner, core],
+                send_sem=give_send.at[offset - 1],
+                recv_sem=give_recv.at[offset - 1],
+                device_id={"seq": chip_peer(offset)},
+                device_id_type=MESH,
+            )
+            got.wait_recv()
+        hand = pltpu.make_async_remote_copy(
+            src_ref=out_ref.at[owner, core],
+            dst_ref=out_ref.at[owner, core],
+            send_sem=hand_send.at[offset],
+            recv_sem=hand_recv.at[offset],
+            device_id={"seq": partner},
+            device_id_type=MESH,
+        )
+        hand.start()
+        hands.append(hand)
+    for copy in gives:
+        copy.wait_send()
+    for offset, hand in enumerate(hands):
+        owner = lax.rem(chip + chips - offset, chips)
+        hand.wait_send()
+        pltpu.make_async_remote_copy(
+            src_ref=out_ref.at[owner, 1 - core],
+            dst_ref=out_ref.at[owner, 1 - core],
+            send_sem=hand_send.at[offset],
+            recv_sem=hand_recv.at[offset],
+            device_id={"seq": partner},
+            device_id_type=MESH,
+        ).wait_recv()
+
+
+def sum_over_mesh(down_shard, up_shard, seq_count, fsdp_count):
+    chips = seq_count // 2
+    rank, width = down_shard.shape
+    blocks = down_shard.reshape(rank, seq_count, SUM_LANES).transpose(1, 0, 2)
+    ups = up_shard.reshape(seq_count, 1, SUM_LANES)
+    parts = jnp.concatenate(
+        [blocks, ups, jnp.zeros((seq_count, SUM_ROWS - rank - 1, SUM_LANES), jnp.float32)], axis=1
+    ).reshape(chips, 2, SUM_ROWS, SUM_LANES)
+    block = (SUM_ROWS, SUM_LANES)
+    sems = pltpu.SemaphoreType.DMA
+    summed = pl.pallas_call(
+        functools.partial(sum_kernel, chips, fsdp_count),
+        out_shape=jax.ShapeDtypeStruct(parts.shape, jnp.float32),
+        in_specs=[pl.BlockSpec(memory_space=pltpu.VMEM)],
+        out_specs=pl.BlockSpec(memory_space=pltpu.VMEM),
+        scratch_shapes=[
+            pltpu.VMEM((chips,) + block, jnp.float32),
+            pltpu.VMEM((chips,) + block, jnp.float32),
+            pltpu.VMEM((chips - 1,) + block, jnp.float32),
+            pltpu.VMEM((1,) + block, jnp.float32),
+            pltpu.VMEM((fsdp_count - 1,) + block, jnp.float32),
+            sems,
+            sems,
+            sems((chips - 1,)),
+            sems((chips - 1,)),
+            sems((fsdp_count - 1,)),
+            sems((fsdp_count - 1,)),
+            sems((chips - 1,)),
+            sems((chips - 1,)),
+            sems((chips,)),
+            sems((chips,)),
+        ],
+        compiler_params=pltpu.CompilerParams(collective_id=0, has_side_effects=True),
+        name="adapter_sum",
+    )(parts).reshape(seq_count, SUM_ROWS, SUM_LANES)
+    down = summed[:, :rank].transpose(1, 0, 2).reshape(rank, width)
+    up = summed[:, rank].reshape(up_shard.shape)
+    return down, up
 
 
 def contract_trailing(left_rows, right_rows):
@@ -170,7 +373,9 @@
         * jnp.dot(adapter_projection.T, value_gradient_matrix, precision=lax.Precision.HIGHEST)
         / overall_token_count
     )
-    adapter_down_gradient, adapter_up_gradient = lax.psum((down_shard, up_shard), ("seq", "fsdp"))
+    adapter_down_gradient, adapter_up_gradient = sum_over_mesh(
+        down_shard, up_shard, seq_count, fsdp_count
+    )
     return (
         input_gradient.reshape(1, token_rows, model_features),
         rotated_query_gradient,

time: 530 us -> 350 us (0.66)
  waiting for transfers between devices: 199 us -> 70.7 us
  blocking collectives: 92.4 us -> 0 us
  Pallas kernels: 0 us -> 51.2 us
  matrix products: 87 us -> 73.3 us
    psum x1 -> x0, waiting for transfers between devices: 149 us -> none  [body(): lax.psum((down_shard, up_shard), ('seq', 'fsdp'))]
    psum x1 -> x0, blocking collectives: 92.4 us -> none  [body(): lax.psum((down_shard, up_shard), ('seq', 'fsdp'))]
    pallas_call x0 -> x1, Pallas kernels: none -> 51.2 us  [sum_over_mesh(): pl.pallas_call(functools.partial(sum_kernel, chips, fsdp_count), out_shap...]
    all_to_all x1, waiting for transfers between devices: 0.01 us -> 22.7 us  [body(): lax.all_to_all(grad_values, 'seq', split_axis=0, concat_axis=1, tiled=True)]
    dot_general x8, matrix products: 22.6 us -> 9.28 us  [body(): jnp.einsum('hqk,qhd->khd', probs_low, grad_block, preferred_element_type=...]
    all_to_all x1, waiting for transfers between devices: 5.48 us -> 0.01 us  [body(): lax.all_to_all(grad_queries, 'seq', split_axis=0, concat_axis=1, tiled=True)]
    unnamed x280 -> x300, local copies, waits for them, and re-layouts: 22.2 us -> 22.4 us
  transfers between devices with their start and end apart: 9 -> 8, of which waited for: 6 -> 5; matrix products, arithmetic and copies ran while one was open for 31% -> 35% of each run, Pallas kernels for 0% -> 15%
where the time goes in v1:
time: 350 us; the launch traced here: 346 us
  matrix products  73.3 us (21%)
  waiting for transfers between devices  70.7 us (20%)
  local copies, waits for them, and re-layouts  63 us (18%)
  Pallas kernels  51.2 us (15%)
  starting transfers between devices  40.4 us (12%)
  other arithmetic  30.6 us (9%)
  between operations  16.3 us (5%)
    pallas_call x1, Pallas kernels, sum_over_mesh(): pl.pallas_call(functools.partial(sum_kernel, chips, fsdp_count), out_shap...  51.2 us
    all_to_all x1, waiting for transfers between devices, body(): lax.all_to_all(grad_values, 'seq', split_axis=0, concat_axis=1, tiled=True)  22.7 us
    unnamed x300, local copies, waits for them, and re-layouts  22.4 us
    dot_general x8, matrix products, body(): jnp.einsum('hqk,qhd->khd', grad_scores, query_block, preferred_element_ty...  20.2 us
    all_to_all x1, waiting for transfers between devices, body(): lax.all_to_all(attention_output_gradient.reshape(shaped), 'seq', split_ax...  16.7 us
    dot_general x8, matrix products, body(): jnp.einsum('qhd,khd->hqk', grad_block, value_block, preferred_element_typ...  15 us
    slice x9, local copies, waits for them, and re-layouts, body(): query_block = head_query[first_row:finish]  13.6 us
    all_to_all x1, waiting for transfers between devices, body(): lax.all_to_all(value_broadcast, 'seq', split_axis=1, concat_axis=0, tiled...  12.9 us
  transfers between devices with their start and end apart: 8, of which 5 were waited for; matrix products, arithmetic and copies ran while one was open for 35% of the time, Pallas kernels for 15%

profile of v1, /device:TPU:1, one launch (start us, length us, event | category | flops | bytes accessed | tf_op | source)
XLA Modules:
  0.0 345.7 jit_solution(2621408974975667352)
XLA Ops:
  7.9 2.3 copy.173
  10.2 8.6 %all-to-all-start.2 = ((bf16[128,32,128]{0,2,1:T(8,128)(2,1)}), bf16[128,32,128]{0,2,1:T(8,128)(2,1)S(1)}, u32[]{:S(2)}, u32[]{:S(2)}) async-start(bf16[128,32,128]{0,2,1:T(8,128)(2,1)} %bitcast.432), calls=%async_computation.2 | async-start | bytes 2097152 | tf_op jit(solution)/shard_map/all_to_all | solution.py:270
  19.2 16.7 %all-to-all-done.2 = bf16[128,32,128]{0,2,1:T(8,128)(2,1)S(1)} async-done(((bf16[128,32,128]{0,2,1:T(8,128)(2,1)}), bf16[128,32,128]{0,2,1:T(8,128)(2,1)S(1)}, u32[]{:S(2)}, u32[]{:S(2)}) %all-to-all-start.2) | async-done | bytes 1048608 | tf_op jit(solution)/shard_map/all_to_all | solution.py:270
  37.2 4.0 %all-to-all-start.1 = ((bf16[128,32,128]{2,0,1:T(8,128)(2,1)}), bf16[128,32,128]{2,0,1:T(8,128)(2,1)S(1)}, u32[]{:S(2)}, u32[]{:S(2)}) async-start(bf16[128,32,128]{2,0,1:T(8,128)(2,1)} %bitcast.430), calls=%async_computation.1 | async-start | bytes 2097152 | tf_op jit(solution)/shard_map/all_to_all | solution.py:268
  49.3 9.1 %all-to-all-done.1 = bf16[128,32,128]{2,0,1:T(8,128)(2,1)S(1)} async-done(((bf16[128,32,128]{2,0,1:T(8,128)(2,1)}), bf16[128,32,128]{2,0,1:T(8,128)(2,1)S(1)}, u32[]{:S(2)}, u32[]{:S(2)}) %all-to-all-start.1) | async-done | bytes 1048608 | tf_op jit(solution)/shard_map/all_to_all | solution.py:268
  58.3 4.8 %all-to-all-start = ((bf16[128,32,128]{0,2,1:T(8,128)(2,1)}), bf16[128,32,128]{0,2,1:T(8,128)(2,1)}, u32[]{:S(2)}, u32[]{:S(2)}) async-start(bf16[128,32,128]{0,2,1:T(8,128)(2,1)} %bitcast.429), calls=%async_computation | async-start | bytes 2097152 | tf_op jit(solution)/shard_map/all_to_all | solution.py:265
  71.4 8.8 %all-to-all-done = bf16[128,32,128]{0,2,1:T(8,128)(2,1)} async-done(((bf16[128,32,128]{0,2,1:T(8,128)(2,1)}), bf16[128,32,128]{0,2,1:T(8,128)(2,1)}, u32[]{:S(2)}, u32[]{:S(2)}) %all-to-all-start) | async-done | bytes 1048608 | tf_op jit(solution)/shard_map/all_to_all | solution.py:265
  80.2 2.3 fusion.117
  128.0 4.9 %all-to-all-start.3 = ((f32[4096,1,128]{2,1,0:T(1,128)}), f32[4096,1,128]{2,1,0:T(1,128)}, u32[]{:S(2)}, u32[]{:S(2)}) async-start(f32[4096,1,128]{2,1,0:T(1,128)} %bitcast.423), calls=%async_computation.3 | async-start | bytes 4194304 | tf_op jit(solution)/shard_map/all_to_all | solution.py:335
  133.5 4.7 %fusion.56 = f32[128,512]{1,0:T(8,128)S(1)} fusion(bf16[8192,512]{1,0:T(8,128)(2,1)} %all-gather.2.cloned.1.call-done, bf16[1,128,8192]{2,1,0:T(8,128)(2,1)S(1)} %copy-done), kind=kOutput, calls=%fused_computation.102 | convolution fusion | flops 1073741824 | bytes 10747904 | tf_op jit(solution)/shard_map/dot_general | solution.py:247
  138.5 22.7 %all-to-all-done.3 = f32[4096,1,128]{2,1,0:T(1,128)} async-done(((f32[4096,1,128]{2,1,0:T(1,128)}), f32[4096,1,128]{2,1,0:T(1,128)}, u32[]{:S(2)}, u32[]{:S(2)}) %all-to-all-start.3) | async-done | bytes 2097184 | tf_op jit(solution)/shard_map/all_to_all | solution.py:335
  162.4 6.3 %all-to-all-start.4 = ((bf16[128,32,128]{2,0,1:T(8,128)(2,1)}), bf16[128,32,128]{2,0,1:T(8,128)(2,1)S(1)}, u32[]{:S(2)}, u32[]{:S(2)}) async-start(bf16[128,32,128]{2,0,1:T(8,128)(2,1)} %bitcast.431), calls=%async_computation.4 | async-start | bytes 2097152 | tf_op jit(solution)/shard_map/all_to_all | solution.py:269
  169.4 2.4 reduce_sum.180
  172.9 12.9 %all-to-all-done.4 = bf16[128,32,128]{2,0,1:T(8,128)(2,1)S(1)} async-done(((bf16[128,32,128]{2,0,1:T(8,128)(2,1)}), bf16[128,32,128]{2,0,1:T(8,128)(2,1)S(1)}, u32[]{:S(2)}, u32[]{:S(2)}) %all-to-all-start.4) | async-done | bytes 1048608 | tf_op jit(solution)/shard_map/all_to_all | solution.py:269
  191.7 3.1 multiply_reduce_fusion.5
  194.9 3.1 multiply_reduce_fusion.4
  207.4 2.7 multiply_convert_fusion.5
  212.0 2.7 multiply_convert_fusion.4
  224.5 2.7 reduce.50
  228.2 4.3 %all-to-all-start.5 = ((bf16[32,2,8192]{2,1,0:T(2,128)(2,1)}), bf16[32,2,8192]{2,1,0:T(2,128)(2,1)S(1)}, u32[]{:S(2)}, u32[]{:S(2)}) async-start(bf16[32,2,8192]{2,1,0:T(2,128)(2,1)} %reshape.820), calls=%async_computation.5 | async-start | bytes 2097152 | tf_op jit(solution)/shard_map/all_to_all | solution.py:331
  232.5 2.6 dynamic_update_slice.56
  235.1 2.7 fusion.71
  237.9 2.8 fusion.37
  240.7 2.8 fusion.35
  243.4 2.8 fusion.33
  246.2 2.8 fusion.31
  249.1 2.7 fusion.29
  251.7 2.6 fusion.27
  254.4 7.5 %all-to-all-start.6 = ((f32[4096,1,128]{2,1,0:T(1,128)}), f32[4096,1,128]{2,1,0:T(1,128)}, u32[]{:S(2)}, u32[]{:S(2)}) async-start(f32[4096,1,128]{2,1,0:T(1,128)} %bitcast.139), calls=%async_computation.6 | async-start | bytes 4194304 | tf_op jit(solution)/shard_map/all_to_all | solution.py:334
  264.1 51.2 %adapter_sum.1 = f32[16,2,24,256]{3,2,1,0:T(8,128)} custom-call(f32[16,2,24,256]{3,2,1,0:T(8,128)} %maximum_maximum_fusion.parts_ref), custom_call_target="tpu_custom_call" | custom-call | tf_op jit(solution)/shard_map/adapter_sum/pallas_call | solution.py:188
  318.9 6.3 %fusion.105 = f32[128,8192]{1,0:T(8,128)S(1)} fusion(bf16[8192,512]{1,0:T(8,128)(2,1)} %all-gather.2.cloned.1.call-done, f32[128,512]{0,1:T(8,128)S(1)} %bitcast.427), kind=kOutput, calls=%fused_computation.179 | convolution fusion | flops 1073807360 | bytes 12845056 | tf_op jit(solution)/shard_map/dot_general | solution.py:219
  327.2 3.5 %reshape.821 = bf16[4096,1,128]{2,1,0:T(2,128)(2,1)} reshape(bf16[32,2,8192]{2,1,0:T(2,128)(2,1)S(1)} %all-to-all-done.5) | data formatting | bytes 2097152
  (415 shorter events, 110.3 us)
Async XLA Ops:
  7.2 125.7 %copy-start = (bf16[1,128,8192]{2,1,0:T(8,128)(2,1)S(1)}, bf16[1,128,8192]{2,1,0:T(8,128)(2,1)}, u32[]{:S(2)}) copy-start(bf16[1,128,8192]{2,1,0:T(8,128)(2,1)} %param.8) | copy-start | bytes 6291460
  7.2 11.6 %copy-start.61 = (bf16[1,128,512]{2,1,0:T(8,128)(2,1)S(1)}, bf16[1,128,512]{2,1,0:T(8,128)(2,1)}, u32[]{:S(2)}) copy-start(bf16[1,128,512]{2,1,0:T(8,128)(2,1)} %param.10) | copy-start | bytes 393220
  7.2 11.7 %copy-start.145 = (s32[1,8]{1,0:T(1,128)S(1)}, s32[1,8]{1,0:T(1,128)}, u32[]{:S(2)}) copy-start(s32[1,8]{1,0:T(1,128)} %param.15) | copy-start | bytes 100
  7.2 126.3 %all-gather.2.cloned.1.call-start = ((), (), s32[]{:S(2)}) async-start(), calls=%async_computation.7 | async-start | bytes 9437184 | tf_op jit(solution)/shard_map/all_gather | solution.py:355
  10.2 25.6 %all-to-all-start.2 = ((bf16[128,32,128]{0,2,1:T(8,128)(2,1)}), bf16[128,32,128]{0,2,1:T(8,128)(2,1)S(1)}, u32[]{:S(2)}, u32[]{:S(2)}) async-start(bf16[128,32,128]{0,2,1:T(8,128)(2,1)} %bitcast.432), calls=%async_computation.2 | async-start | bytes 2097152 | tf_op jit(solution)/shard_map/all_to_all | solution.py:270
  19.2 46.4 %copy-start.47 = (s32[4096]{0:T(1024)}, s32[4096]{0:T(1024)S(1)}, u32[]{:S(2)}) copy-start(s32[4096]{0:T(1024)S(1)} %convert_reduce_fusion) | copy-start | bytes 49156
  37.2 21.1 %all-to-all-start.1 = ((bf16[128,32,128]{2,0,1:T(8,128)(2,1)}), bf16[128,32,128]{2,0,1:T(8,128)(2,1)S(1)}, u32[]{:S(2)}, u32[]{:S(2)}) async-start(bf16[128,32,128]{2,0,1:T(8,128)(2,1)} %bitcast.430), calls=%async_computation.1 | async-start | bytes 2097152 | tf_op jit(solution)/shard_map/all_to_all | solution.py:268
  58.3 21.9 %all-to-all-start = ((bf16[128,32,128]{0,2,1:T(8,128)(2,1)}), bf16[128,32,128]{0,2,1:T(8,128)(2,1)}, u32[]{:S(2)}, u32[]{:S(2)}) async-start(bf16[128,32,128]{0,2,1:T(8,128)(2,1)} %bitcast.429), calls=%async_computation | async-start | bytes 2097152 | tf_op jit(solution)/shard_map/all_to_all | solution.py:265
  69.8 33.1 %copy-start.130 = (s32[512]{0:T(512)S(1)}, s32[512]{0:T(512)}, u32[]{:S(2)}) copy-start(s32[512]{0:T(512)} %get-tuple-element.55) | copy-start | bytes 6148
  69.8 33.1 %copy-start.131 = (s32[512]{0:T(512)S(1)}, s32[512]{0:T(512)}, u32[]{:S(2)}) copy-start(s32[512]{0:T(512)} %get-tuple-element.94) | copy-start | bytes 6148
  91.0 18.7 %copy-start.35 = (bf16[4,128,1,128]{3,1,0,2:T(8,128)(2,1)}, bf16[4,128,1,128]{3,1,0,2:T(8,128)(2,1)S(1)}, u32[]{:S(2)}) copy-start(bf16[4,128,1,128]{3,1,0,2:T(8,128)(2,1)S(1)} %copy.179) | copy-start | bytes 393220
  92.9 18.5 %copy-start.37 = (bf16[4,128,1,128]{3,1,0,2:T(8,128)(2,1)}, bf16[4,128,1,128]{3,1,0,2:T(8,128)(2,1)S(1)}, u32[]{:S(2)}) copy-start(bf16[4,128,1,128]{3,1,0,2:T(8,128)(2,1)S(1)} %copy.181) | copy-start | bytes 393220
  106.9 11.4 %copy-start.14 = (f32[512,1024]{1,0:T(8,128)}, f32[512,1024]{1,0:T(8,128)S(1)}, u32[]{:S(2)}) copy-start(f32[512,1024]{1,0:T(8,128)S(1)} %get-tuple-element.65) | copy-start | bytes 6291460
  108.1 8.3 %copy-start.48 = (bf16[12,128,1,128]{3,1,0,2:T(8,128)(2,1)}, bf16[12,128,1,128]{3,1,0,2:T(8,128)(2,1)S(1)}, u32[]{:S(2)}) copy-start(bf16[12,128,1,128]{3,1,0,2:T(8,128)(2,1)S(1)} %get-tuple-element.26) | copy-start | bytes 1179652
  109.1 10.0 %copy-start.11 = (f32[512,1536]{1,0:T(8,128)}, f32[512,1536]{1,0:T(8,128)S(1)}, u32[]{:S(2)}) copy-start(f32[512,1536]{1,0:T(8,128)S(1)} %get-tuple-element.67) | copy-start | bytes 9437188
  109.1 10.0 %copy-start.106 = (f32[512]{0:T(512)}, f32[512]{0:T(512)S(1)}, u32[]{:S(2)}) copy-start(f32[512]{0:T(512)S(1)} %get-tuple-element.66) | copy-start | bytes 6148
  109.7 9.5 %copy-start.120 = (f32[512]{0:T(512)}, f32[512]{0:T(512)S(1)}, u32[]{:S(2)}) copy-start(f32[512]{0:T(512)S(1)} %fusion.9) | copy-start | bytes 6148
  110.8 9.7 %copy-start.9 = (f32[512,1536]{1,0:T(8,128)}, f32[512,1536]{1,0:T(8,128)S(1)}, u32[]{:S(2)}) copy-start(f32[512,1536]{1,0:T(8,128)S(1)} %get-tuple-element.69) | copy-start | bytes 9437188
  110.8 9.7 %copy-start.104 = (f32[512]{0:T(512)}, f32[512]{0:T(512)S(1)}, u32[]{:S(2)}) copy-start(f32[512]{0:T(512)S(1)} %get-tuple-element.68) | copy-start | bytes 6148
  111.4 9.2 %copy-start.117 = (f32[512]{0:T(512)}, f32[512]{0:T(512)S(1)}, u32[]{:S(2)}) copy-start(f32[512]{0:T(512)S(1)} %fusion.11) | copy-start | bytes 6148
  112.5 9.3 %copy-start.5 = (f32[512,1536]{1,0:T(8,128)}, f32[512,1536]{1,0:T(8,128)S(1)}, u32[]{:S(2)}) copy-start(f32[512,1536]{1,0:T(8,128)S(1)} %get-tuple-element.71) | copy-start | bytes 9437188
  112.5 9.3 %copy-start.100 = (f32[512]{0:T(512)}, f32[512]{0:T(512)S(1)}, u32[]{:S(2)}) copy-start(f32[512]{0:T(512)S(1)} %get-tuple-element.70) | copy-start | bytes 6148
  113.1 8.7 %copy-start.112 = (f32[512]{0:T(512)}, f32[512]{0:T(512)S(1)}, u32[]{:S(2)}) copy-start(f32[512]{0:T(512)S(1)} %fusion.13) | copy-start | bytes 6148
  114.1 8.8 %copy-start.3 = (f32[512,1536]{1,0:T(8,128)}, f32[512,1536]{1,0:T(8,128)S(1)}, u32[]{:S(2)}) copy-start(f32[512,1536]{1,0:T(8,128)S(1)} %get-tuple-element.73) | copy-start | bytes 9437188
  114.1 8.8 %copy-start.98 = (f32[512]{0:T(512)}, f32[512]{0:T(512)S(1)}, u32[]{:S(2)}) copy-start(f32[512]{0:T(512)S(1)} %get-tuple-element.72) | copy-start | bytes 6148
  115.8 8.4 %copy-start.1 = (f32[512,1536]{1,0:T(8,128)}, f32[512,1536]{1,0:T(8,128)S(1)}, u32[]{:S(2)}) copy-start(f32[512,1536]{1,0:T(8,128)S(1)} %get-tuple-element.75) | copy-start | bytes 9437188
  115.8 8.4 %copy-start.96 = (f32[512]{0:T(512)}, f32[512]{0:T(512)S(1)}, u32[]{:S(2)}) copy-start(f32[512]{0:T(512)S(1)} %get-tuple-element.74) | copy-start | bytes 6148
  128.0 33.2 %all-to-all-start.3 = ((f32[4096,1,128]{2,1,0:T(1,128)}), f32[4096,1,128]{2,1,0:T(1,128)}, u32[]{:S(2)}, u32[]{:S(2)}) async-start(f32[4096,1,128]{2,1,0:T(1,128)} %bitcast.423), calls=%async_computation.3 | async-start | bytes 4194304 | tf_op jit(solution)/shard_map/all_to_all | solution.py:335
  162.4 23.4 %all-to-all-start.4 = ((bf16[128,32,128]{2,0,1:T(8,128)(2,1)}), bf16[128,32,128]{2,0,1:T(8,128)(2,1)S(1)}, u32[]{:S(2)}, u32[]{:S(2)}) async-start(bf16[128,32,128]{2,0,1:T(8,128)(2,1)} %bitcast.431), calls=%async_computation.4 | async-start | bytes 2097152 | tf_op jit(solution)/shard_map/all_to_all | solution.py:269
  228.2 26.1 %all-to-all-start.5 = ((bf16[32,2,8192]{2,1,0:T(2,128)(2,1)}), bf16[32,2,8192]{2,1,0:T(2,128)(2,1)S(1)}, u32[]{:S(2)}, u32[]{:S(2)}) async-start(bf16[32,2,8192]{2,1,0:T(2,128)(2,1)} %reshape.820), calls=%async_computation.5 | async-start | bytes 2097152 | tf_op jit(solution)/shard_map/all_to_all | solution.py:331
  251.7 10.6 %copy-start.79 = (bf16[16,512]{1,0:T(8,128)(2,1)S(1)}, bf16[16,512]{1,0:T(8,128)(2,1)}, u32[]{:S(2)}) copy-start(bf16[16,512]{1,0:T(8,128)(2,1)} %param.14) | copy-start | bytes 49156
  254.4 81.6 %all-to-all-start.6 = ((f32[4096,1,128]{2,1,0:T(1,128)}), f32[4096,1,128]{2,1,0:T(1,128)}, u32[]{:S(2)}, u32[]{:S(2)}) async-start(f32[4096,1,128]{2,1,0:T(1,128)} %bitcast.139), calls=%async_computation.6 | async-start | bytes 4194304 | tf_op jit(solution)/shard_map/all_to_all | solution.py:334
  (123 other events, 313.3 us)
Sparse Core Ops, SparseCore 0:
  9.8 97.6 all-gather.1

commit v2 on v1

--- a/solution.py
+++ b/solution.py
@@ -8,12 +8,13 @@
 from jax.sharding import PartitionSpec as P
 
 HEAD_FEATURES = 128
-QUERY_HEADS = 32
-KEY_VALUE_HEADS = 4
 
 
 ADAPTER_SCALE = 2.0
 NEG_FILL = -1e30
+LOG2_E = 1.4426950408889634
+DOCS = 8
+DOC_MOST = 1024
 
 
 MESH = pl.DeviceIdType.MESH
@@ -215,6 +216,521 @@
     return down, up
 
 
+def halo_copies(source_ref, target_ref, send_sems, recv_sems, chips, reach):
+    me = lax.axis_index("seq")
+    chip = me // 2
+    core = lax.rem(me, 2)
+    rows, width = source_ref.shape
+    half = width // 2
+    own = None
+    remote = []
+    for behind in range(reach + 1):
+        for cross in range(2):
+            to_core = core if cross == 0 else 1 - core
+            lanes = pl.ds(pl.multiple_of(to_core * half, half), half)
+            slot = pl.multiple_of(((reach - behind) * 2 + core) * rows, rows)
+            source = source_ref.at[:, lanes]
+            target = target_ref.at[pl.ds(slot, rows), :]
+            index = behind * 2 + cross
+            if index == 0:
+                own = pltpu.make_async_copy(source, target, send_sems.at[0])
+            else:
+                remote.append(
+                    pltpu.make_async_remote_copy(
+                        src_ref=source,
+                        dst_ref=target,
+                        send_sem=send_sems.at[index],
+                        recv_sem=recv_sems.at[index],
+                        device_id={"seq": lax.rem(chip + behind, chips) * 2 + to_core},
+                        device_id_type=MESH,
+                    )
+                )
+    return own, remote
+
+
+def greet_halo(barrier, chips, reach, step):
+    me = lax.axis_index("seq")
+    chip = me // 2
+    core = lax.rem(me, 2)
+    for away in range(reach + 1):
+        for cross in range(2):
+            if away == 0 and cross == 0:
+                continue
+            to_core = core if cross == 0 else 1 - core
+            peer = lax.rem(chip + chips + step * away, chips) * 2 + to_core
+            pl.semaphore_signal(barrier, inc=1, device_id={"seq": peer}, device_id_type=MESH)
+
+
+def gather_kernel(
+    chips,
+    depth,
+    reach,
+    q_ref,
+    o_ref,
+    k_ref,
+    w_ref,
+    qc_ref,
+    oc_ref,
+    kc_ref,
+    wc_ref,
+    halo_send,
+    halo_recv,
+    pair_send,
+    pair_recv,
+    local_sem,
+    ring_send,
+    ring_recv,
+    hand_send,
+    hand_recv,
+):
+    me = lax.axis_index("seq")
+    layer = lax.axis_index("fsdp")
+    core = lax.rem(me, 2)
+    partner = me + 1 - 2 * core
+    up = lax.rem(layer + 1, depth)
+    down = lax.rem(layer + depth - 1, depth)
+
+    barrier = pltpu.get_barrier_semaphore()
+    greet_halo(barrier, chips, reach, -1)
+    for peer in (up, down):
+        pl.semaphore_signal(barrier, inc=1, device_id={"fsdp": peer}, device_id_type=MESH)
+    pl.semaphore_wait(barrier, 2 * reach + 3)
+
+    shard = w_ref.shape[0]
+    half = shard // 2
+    quarter = half // 2
+    steps = depth // 2
+
+    def ring_rows(block, step, way):
+        first = block * shard + core * half
+        if step < steps:
+            return pl.ds(pl.multiple_of(first, half), half)
+        return pl.ds(pl.multiple_of(first + way * quarter, quarter), quarter)
+
+    def ring_copy(step, way):
+        if way == 0:
+            block, peer = lax.rem(layer + depth - (step - 1), depth), up
+        else:
+            block, peer = lax.rem(layer + (step - 1), depth), down
+        rows = ring_rows(block, step, way)
+        if step == 1:
+            first = core * half
+            source = w_ref.at[pl.ds(pl.multiple_of(first, half), half), :]
+            rows = pl.ds(pl.multiple_of(block * shard + first, half), half)
+        else:
+            source = wc_ref.at[rows, :]
+        return pltpu.make_async_remote_copy(
+            src_ref=source,
+            dst_ref=wc_ref.at[rows, :],
+            send_sem=ring_send.at[way, step - 1],
+            recv_sem=ring_recv.at[way, step - 1],
+            device_id={"fsdp": peer},
+            device_id_type=MESH,
+        )
+
+    def hand_copy(step, way, sender):
+        block = lax.rem(layer + depth + (step if way else -step), depth)
+        first = block * shard + sender * half
+        if step < steps:
+            rows = pl.ds(pl.multiple_of(first, half), half)
+        else:
+            rows = pl.ds(pl.multiple_of(first + way * quarter, quarter), quarter)
+        return pltpu.make_async_remote_copy(
+            src_ref=wc_ref.at[rows, :],
+            dst_ref=wc_ref.at[rows, :],
+            send_sem=hand_send.at[way, step - 1],
+            recv_sem=hand_recv.at[way, step - 1],
+            device_id={"seq": partner},
+            device_id_type=MESH,
+        )
+
+    def got_copy(step, way):
+        block = lax.rem(layer + depth + (step if way else -step), depth)
+        rows = ring_rows(block, step, way)
+        return pltpu.make_async_remote_copy(
+            src_ref=wc_ref.at[rows, :],
+            dst_ref=wc_ref.at[rows, :],
+            send_sem=ring_send.at[way, step - 1],
+            recv_sem=ring_recv.at[way, step - 1],
+            device_id={"fsdp": up},
+            device_id_type=MESH,
+        )
+
+    sent = []
+    for way in range(2):
+        copy = ring_copy(1, way)
+        copy.start()
+        sent.append(copy)
+
+    own_key, keys = halo_copies(k_ref, kc_ref, halo_send, halo_recv, chips, reach)
+    for copy in keys:
+        copy.start()
+    own_key.start()
+    rows = q_ref.shape[0]
+    wide = q_ref.shape[1] // 2
+    here = pl.ds(pl.multiple_of(core * rows, rows), rows)
+    mine = pl.ds(pl.multiple_of(core * wide, wide), wide)
+    theirs = pl.ds(pl.multiple_of((1 - core) * wide, wide), wide)
+    pairs = []
+    locals_ = [own_key]
+    for index, (source_ref, target_ref) in enumerate(((q_ref, qc_ref), (o_ref, oc_ref))):
+        copy = pltpu.make_async_remote_copy(
+            src_ref=source_ref.at[:, theirs],
+            dst_ref=target_ref.at[here, :],
+            send_sem=pair_send.at[index],
+            recv_sem=pair_recv.at[index],
+            device_id={"seq": partner},
+            device_id_type=MESH,
+        )
+        copy.start()
+        pairs.append(copy)
+        copy = pltpu.make_async_copy(
+            source_ref.at[:, mine], target_ref.at[here, :], local_sem.at[index]
+        )
+        copy.start()
+        locals_.append(copy)
+    copy = pltpu.make_async_copy(
+        w_ref,
+        wc_ref.at[pl.ds(pl.multiple_of(layer * shard, shard), shard), :],
+        local_sem.at[2],
+    )
+    copy.start()
+    locals_.append(copy)
+
+    hands = []
+    for step in range(1, steps + 1):
+        for way in range(2):
+            got_copy(step, way).wait_recv()
+            if step < steps:
+                copy = ring_copy(step + 1, way)
+                copy.start()
+                sent.append(copy)
+            copy = hand_copy(step, way, core)
+            copy.start()
+            hands.append(copy)
+    for copy in locals_:
+        copy.wait()
+    for copy in sent:
+        copy.wait_send()
+    for copy in hands:
+        copy.wait_send()
+    for step in range(1, steps + 1):
+        for way in range(2):
+            hand_copy(step, way, 1 - core).wait_recv()
+    for copy in keys:
+        copy.wait()
+    for copy in pairs:
+        copy.wait()
+
+
+def gather_all(queries, grads, keys, weight, chips, depth, reach):
+    rows, width = queries.shape
+    kv = keys.shape[1]
+    sems = pltpu.SemaphoreType.DMA
+    links = 2 * (reach + 1)
+    anywhere = pl.BlockSpec(memory_space=pl.ANY)
+    vmem = pl.BlockSpec(memory_space=pltpu.VMEM)
+    dtype = jnp.bfloat16
+    return pl.pallas_call(
+        functools.partial(gather_kernel, chips, depth, reach),
+        out_shape=(
+            jax.ShapeDtypeStruct((2 * rows, width // 2), dtype),
+            jax.ShapeDtypeStruct((2 * rows, width // 2), dtype),
+            jax.ShapeDtypeStruct((links * rows, kv // 2), dtype),
+            jax.ShapeDtypeStruct((depth * weight.shape[0], weight.shape[1]), dtype),
+        ),
+        in_specs=[vmem] * 4,
+        out_specs=(anywhere,) * 4,
+        scratch_shapes=[
+            sems((links,)),
+            sems((links,)),
+            sems((2,)),
+            sems((2,)),
+            sems((3,)),
+            sems((2, depth // 2)),
+            sems((2, depth // 2)),
+            sems((2, depth // 2)),
+            sems((2, depth // 2)),
+        ],
+        compiler_params=pltpu.CompilerParams(collective_id=1, has_side_effects=True),
+        name="gather_inputs",
+    )(queries, grads, keys, weight)
+
+
+def halo_kernel(chips, reach, v_ref, vc_ref, send_sems, recv_sems):
+    barrier = pltpu.get_barrier_semaphore()
+    greet_halo(barrier, chips, reach, -1)
+    pl.semaphore_wait(barrier, 2 * reach + 1)
+    own, remote = halo_copies(v_ref, vc_ref, send_sems, recv_sems, chips, reach)
+    for copy in remote:
+        copy.start()
+    own.start()
+    own.wait()
+    for copy in remote:
+        copy.wait()
+
+
+def gather_values(values, chips, reach):
+    rows, kv = values.shape
+    links = 2 * (reach + 1)
+    sems = pltpu.SemaphoreType.DMA
+    return pl.pallas_call(
+        functools.partial(halo_kernel, chips, reach),
+        out_shape=jax.ShapeDtypeStruct((links * rows, kv // 2), values.dtype),
+        in_specs=[pl.BlockSpec(memory_space=pltpu.VMEM)],
+        out_specs=pl.BlockSpec(memory_space=pl.ANY),
+        scratch_shapes=[sems((links,)), sems((links,))],
+        compiler_params=pltpu.CompilerParams(collective_id=2, has_side_effects=True),
+        name="gather_values",
+    )(values)
+
+
+def attention_kernel(
+    info_ref,
+    q_ref,
+    o_ref,
+    k_ref,
+    v_ref,
+    dq_ref,
+    dkv_ref,
+    bias_ref,
+    s_ref,
+    g_ref,
+    p_ref,
+    d_ref,
+    acc_ref,
+):
+    chip = info_ref[0]
+    side = pl.program_id(1)
+    rows = q_ref.shape[0]
+    heads = q_ref.shape[1] // HEAD_FEATURES
+    window = bias_ref.shape[0]
+    span = k_ref.shape[0]
+    start = pl.multiple_of(side * rows, rows)
+    inverse = HEAD_FEATURES ** (-0.5)
+    steep = inverse * LOG2_E
+    chunk = 128
+    count = window // chunk
+
+    @pl.when(side == 0)
+    def _():
+        acc_ref[...] = jnp.zeros_like(acc_ref)
+
+    q_place = chip * (2 * rows) + start + lax.broadcasted_iota(jnp.int32, (1, rows), 1)
+    finish = jnp.int32(0)
+    opening = jnp.zeros((1, rows), jnp.int32)
+    for index in range(DOCS):
+        finish = finish + info_ref[1 + index]
+        opening = jnp.where(q_place >= finish, finish, opening)
+    for part in range(count):
+        k_place = (
+            chip * (2 * rows)
+            - (span - 2 * rows)
+            + start
+            + part * chunk
+            + lax.broadcasted_iota(jnp.int32, (chunk, rows), 0)
+        )
+        allowed = (k_place >= opening) & (k_place <= q_place)
+        bias_ref[part * chunk : (part + 1) * chunk, :] = jnp.where(allowed, 0.0, NEG_FILL)
+
+    def stack(ref, first, number):
+        return jnp.concatenate(
+            [
+                ref[:, (first + i) * HEAD_FEATURES : (first + i + 1) * HEAD_FEATURES]
+                for i in range(number)
+            ],
+            axis=0,
+        )
+
+    def fold(values):
+        return values.reshape(chunk // 8, 8, values.shape[1])
+
+    trailing = (((1,), (1,)), ((), ()))
+    for pair in range(heads // 2):
+        q_pair = stack(q_ref, 2 * pair, 2)
+        o_pair = stack(o_ref, 2 * pair, 2)
+        lanes = slice(pair * 2 * rows, (pair + 1) * 2 * rows)
+        peak = None
+        for part in range(count):
+            here = slice(part * chunk, (part + 1) * chunk)
+            scores = lax.dot_general(
+                k_ref[pl.ds(start + part * chunk, chunk), :],
+                q_pair,
+                trailing,
+                preferred_element_type=jnp.float32,
+            )
+            bias = bias_ref[here, :]
+            scores = scores + jnp.concatenate([bias, bias], axis=1)
+            s_ref[here, :] = scores
+            high = jnp.max(fold(scores), axis=0)
+            peak = high if peak is None else jnp.maximum(peak, high)
+        peak = jnp.max(peak, axis=0, keepdims=True)
+        total = jnp.zeros((8, 2 * rows), jnp.float32)
+        delta = jnp.zeros((8, 2 * rows), jnp.float32)
+        for part in range(count):
+            here = slice(part * chunk, (part + 1) * chunk)
+            weights = jnp.exp2((s_ref[here, :] - peak) * steep)
+            grad_probs = lax.dot_general(
+                v_ref[pl.ds(start + part * chunk, chunk), :],
+                o_pair,
+                trailing,
+                preferred_element_type=jnp.float32,
+            )
+            total = total + jnp.sum(fold(weights), axis=0)
+            delta = delta + jnp.sum(fold(weights * grad_probs), axis=0)
+            s_ref[here, :] = weights
+            g_ref[here, :] = grad_probs
+        scale = 1.0 / jnp.sum(total, axis=0, keepdims=True)
+        delta = jnp.sum(delta, axis=0, keepdims=True) * scale
+        for part in range(count):
+            here = slice(part * chunk, (part + 1) * chunk)
+            probs = s_ref[here, :] * scale
+            p_ref[here, lanes] = probs.astype(jnp.bfloat16)
+            d_ref[here, lanes] = (probs * (g_ref[here, :] - delta)).astype(jnp.bfloat16)
+
+    rows_here = pl.ds(start, window)
+    acc_ref[0, rows_here, :] += inverse * jnp.dot(
+        d_ref[...], stack(q_ref, 0, heads), preferred_element_type=jnp.float32
+    )
+    acc_ref[1, rows_here, :] += jnp.dot(
+        p_ref[...], stack(o_ref, 0, heads), preferred_element_type=jnp.float32
+    )
+    grad_t = lax.dot_general(
+        k_ref[rows_here, :],
+        d_ref[...],
+        (((0,), (0,)), ((), ())),
+        preferred_element_type=jnp.float32,
+    )
+    for head in range(heads):
+        block = grad_t[:, head * rows : (head + 1) * rows]
+        dq_ref[:, head * HEAD_FEATURES : (head + 1) * HEAD_FEATURES] = (
+            block.T * inverse
+        ).astype(jnp.bfloat16)
+
+    @pl.when(side == 1)
+    def _():
+        dkv_ref[...] = acc_ref[...].astype(jnp.bfloat16)
+
+
+def attend(info, queries, grads, keys, values):
+    tokens, width = queries.shape
+    rows = tokens // 2
+    span, kv = keys.shape
+    groups = kv // HEAD_FEATURES
+    wide = width // groups
+    window = span - rows
+    stacked = rows * wide // HEAD_FEATURES
+    query_spec = pl.BlockSpec((rows, wide), lambda group, side, info_ref: (side, group))
+    key_spec = pl.BlockSpec((span, HEAD_FEATURES), lambda group, side, info_ref: (0, group))
+    return pl.pallas_call(
+        attention_kernel,
+        grid_spec=pltpu.PrefetchScalarGridSpec(
+            num_scalar_prefetch=1,
+            grid=(groups, 2),
+            in_specs=[query_spec, query_spec, key_spec, key_spec],
+            out_specs=(
+                query_spec,
+                pl.BlockSpec(
+                    (2, span, HEAD_FEATURES), lambda group, side, info_ref: (0, 0, group)
+                ),
+            ),
+            scratch_shapes=[
+                pltpu.VMEM((window, rows), jnp.float32),
+                pltpu.VMEM((window, 2 * rows), jnp.float32),
+                pltpu.VMEM((window, 2 * rows), jnp.float32),
+                pltpu.VMEM((window, stacked), jnp.bfloat16),
+                pltpu.VMEM((window, stacked), jnp.bfloat16),
+                pltpu.VMEM((2, span, HEAD_FEATURES), jnp.float32),
+            ],
+        ),
+        out_shape=(
+            jax.ShapeDtypeStruct((tokens, width), jnp.bfloat16),
+            jax.ShapeDtypeStruct((2, span, kv), jnp.bfloat16),
+        ),
+        name="attention_backward",
+    )(info, queries, grads, keys, values)
+
+
+def return_kernel(
+    chips, reach, dq_ref, dkv_ref, full_ref, parts_ref, send_sems, recv_sems, pair_send, pair_recv, local_sem
+):
+    me = lax.axis_index("seq")
+    chip = me // 2
+    core = lax.rem(me, 2)
+    partner = me + 1 - 2 * core
+    barrier = pltpu.get_barrier_semaphore()
+    greet_halo(barrier, chips, reach, 1)
+    pl.semaphore_wait(barrier, 2 * reach + 1)
+
+    rows = full_ref.shape[0]
+    wide = dq_ref.shape[1]
+    half = dkv_ref.shape[2]
+    kv_lanes = pl.ds(pl.multiple_of(core * half, half), half)
+    waits = []
+    for behind in range(reach, -1, -1):
+        for cross in range(2):
+            to_core = core if cross == 0 else 1 - core
+            slot = pl.multiple_of(((reach - behind) * 2 + to_core) * rows, rows)
+            source = dkv_ref.at[:, pl.ds(slot, rows), :]
+            target = parts_ref.at[behind, :, :, kv_lanes]
+            index = behind * 2 + cross
+            if index == 0:
+                copy = pltpu.make_async_copy(source, target, local_sem.at[0])
+            else:
+                copy = pltpu.make_async_remote_copy(
+                    src_ref=source,
+                    dst_ref=target,
+                    send_sem=send_sems.at[index],
+                    recv_sem=recv_sems.at[index],
+                    device_id={"seq": lax.rem(chip + chips - behind, chips) * 2 + to_core},
+                    device_id_type=MESH,
+                )
+            copy.start()
+            waits.append(copy)
+    lanes = pl.ds(pl.multiple_of(core * wide, wide), wide)
+    copy = pltpu.make_async_remote_copy(
+        src_ref=dq_ref.at[pl.ds(pl.multiple_of((1 - core) * rows, rows), rows), :],
+        dst_ref=full_ref.at[:, lanes],
+        send_sem=pair_send,
+        recv_sem=pair_recv,
+        device_id={"seq": partner},
+        device_id_type=MESH,
+    )
+    copy.start()
+    waits.append(copy)
+    copy = pltpu.make_async_copy(
+        dq_ref.at[pl.ds(pl.multiple_of(core * rows, rows), rows), :],
+        full_ref.at[:, lanes],
+        local_sem.at[1],
+    )
+    copy.start()
+    waits.append(copy)
+    for copy in waits:
+        copy.wait()
+
+
+def give_back(grad_queries, grad_pairs, chips, reach):
+    tokens, width = grad_queries.shape
+    kv = grad_pairs.shape[2]
+    rows = tokens // 2
+    links = 2 * (reach + 1)
+    sems = pltpu.SemaphoreType.DMA
+    anywhere = pl.BlockSpec(memory_space=pl.ANY)
+    vmem = pl.BlockSpec(memory_space=pltpu.VMEM)
+    return pl.pallas_call(
+        functools.partial(return_kernel, chips, reach),
+        out_shape=(
+            jax.ShapeDtypeStruct((rows, 2 * width), jnp.bfloat16),
+            jax.ShapeDtypeStruct((reach + 1, 2, rows, 2 * kv), jnp.bfloat16),
+        ),
+        in_specs=[vmem, vmem],
+        out_specs=(anywhere, anywhere),
+        scratch_shapes=[sems((links,)), sems((links,)), sems, sems, sems((2,))],
+        compiler_params=pltpu.CompilerParams(collective_id=3, has_side_effects=True),
+        name="return_gradients",
+    )(grad_queries, grad_pairs)
+
+
 def contract_trailing(left_rows, right_rows):
     return lax.dot_general(
         left_rows, right_rows, (((1,), (1,)), ((), ())), preferred_element_type=jnp.float32
@@ -236,128 +752,39 @@
     hidden_activations = normed_block_input.reshape(token_rows, model_features)
     seq_count = lax.axis_size("seq")
     fsdp_count = lax.axis_size("fsdp")
-    queries_per_group = QUERY_HEADS // KEY_VALUE_HEADS
-    key_value_features = KEY_VALUE_HEADS * HEAD_FEATURES
-    inverse = HEAD_FEATURES ** (-0.5)
+    chips = seq_count // 2
+    reach = DOC_MOST // (2 * token_rows)
+    up_widened = adapter_up_weight.astype(jnp.float32)
+
+    queries, grads, keys, weight = gather_all(
+        stored_rotated_queries[0],
+        attention_output_gradient[0],
+        stored_rotated_keys[0],
+        frozen_value_weight,
+        chips,
+        fsdp_count,
+        reach,
+    )
     adapter_projection = contract_trailing(hidden_activations, adapter_down_weight)
-    up_widened = adapter_up_weight.astype(jnp.float32)
     adapter_maps = ADAPTER_SCALE * jnp.dot(
         adapter_projection, up_widened, precision=lax.Precision.HIGHEST
     )
-    base_value = jnp.dot(
-        hidden_activations,
-        lax.all_gather(frozen_value_weight, "fsdp", axis=0, tiled=True),
-        preferred_element_type=jnp.float32,
-    )
+    base_value = jnp.dot(hidden_activations, weight, preferred_element_type=jnp.float32)
     adapter_values = (base_value + adapter_maps).astype(jnp.bfloat16)
-    shaped = (token_rows, QUERY_HEADS, HEAD_FEATURES)
-    key_broadcast = jnp.repeat(
-        stored_rotated_keys.reshape(token_rows, KEY_VALUE_HEADS, HEAD_FEATURES),
-        queries_per_group,
-        axis=1,
-    )
-    value_broadcast = jnp.repeat(
-        adapter_values.reshape(token_rows, KEY_VALUE_HEADS, HEAD_FEATURES),
-        queries_per_group,
-        axis=1,
-    )
-    head_query, head_key, head_value, head_grad = (
-        lax.all_to_all(
-            stored_rotated_queries.reshape(shaped), "seq", split_axis=1, concat_axis=0, tiled=True
-        ),
-        lax.all_to_all(key_broadcast, "seq", split_axis=1, concat_axis=0, tiled=True),
-        lax.all_to_all(value_broadcast, "seq", split_axis=1, concat_axis=0, tiled=True),
-        lax.all_to_all(
-            attention_output_gradient.reshape(shaped),
-            "seq",
-            split_axis=1,
-            concat_axis=0,
-            tiled=True,
-        ),
-    )
-    seq_len = head_query.shape[0]
-    local_heads = head_query.shape[1]
-    block_rows = min(512, seq_len)
-    key_reach = block_rows + seq_len // 4
-    bounds = jnp.cumsum(packed_document_lengths[0])
-    places = jnp.arange(seq_len, dtype=jnp.int32)
-    segments = jnp.sum((places[:, None] >= bounds[None, :]).astype(jnp.int32), axis=1)
-    grad_keys = jnp.zeros((seq_len, local_heads, HEAD_FEATURES), jnp.float32)
-    grad_values = jnp.zeros((seq_len, local_heads, HEAD_FEATURES), jnp.float32)
-    query_parts = []
-    for block_index in range(seq_len // block_rows):
-        first_row = block_index * block_rows
-        finish = first_row + block_rows
-        opening = max(0, finish - key_reach)
-        query_block = head_query[first_row:finish]
-        grad_block = head_grad[first_row:finish]
-        key_block = head_key[opening:finish]
-        value_block = head_value[opening:finish]
-        scores = (
-            jnp.einsum("qhd,khd->hqk", query_block, key_block, preferred_element_type=jnp.float32)
-            * inverse
-        )
-        allowed = (places[opening:finish][None, :] <= places[first_row:finish][:, None]) & (
-            segments[opening:finish][None, :] == segments[first_row:finish][:, None]
-        )
-        scores = jnp.where(allowed[None], scores, NEG_FILL)
-        row_peak = jnp.max(scores, axis=2, keepdims=True)
-        weights = jnp.exp(scores - row_peak)
-        probs_full = weights / jnp.sum(weights, axis=2, keepdims=True)
-        probs_low = probs_full.astype(jnp.bfloat16)
-        grad_probs = jnp.einsum(
-            "qhd,khd->hqk", grad_block, value_block, preferred_element_type=jnp.float32
-        )
-        row_delta = jnp.sum(probs_full * grad_probs, axis=2, keepdims=True)
-        grad_scores = (probs_full * (grad_probs - row_delta)).astype(jnp.bfloat16)
-        query_parts.append(
-            jnp.einsum("hqk,khd->qhd", grad_scores, key_block, preferred_element_type=jnp.float32)
-            * inverse
-        )
-        key_part = (
-            jnp.einsum("hqk,qhd->khd", grad_scores, query_block, preferred_element_type=jnp.float32)
-            * inverse
-        )
-        value_part = jnp.einsum(
-            "hqk,qhd->khd", probs_low, grad_block, preferred_element_type=jnp.float32
-        )
-        grad_keys = lax.dynamic_update_slice_in_dim(
-            grad_keys, grad_keys[opening:finish] + key_part, opening, 0
-        )
-        grad_values = lax.dynamic_update_slice_in_dim(
-            grad_values, grad_values[opening:finish] + value_part, opening, 0
-        )
-    grad_queries = jnp.concatenate(query_parts, axis=0).astype(jnp.bfloat16)
-    token_query = lax.all_to_all(grad_queries, "seq", split_axis=0, concat_axis=1, tiled=True)
-    rotated_query_gradient = token_query.reshape(1, token_rows, QUERY_HEADS * HEAD_FEATURES)
-    token_key_matrix, token_value_matrix = (
-        lax.all_to_all(grad_keys, "seq", split_axis=0, concat_axis=1, tiled=True),
-        lax.all_to_all(grad_values, "seq", split_axis=0, concat_axis=1, tiled=True),
-    )
-    per_key_value_head = token_key_matrix.shape[1] // KEY_VALUE_HEADS
-    rotated_key_gradient = (
-        token_key_matrix.reshape(token_rows, KEY_VALUE_HEADS, per_key_value_head, HEAD_FEATURES)
-        .sum(axis=2)
-        .reshape(1, token_rows, key_value_features)
-        .astype(jnp.bfloat16)
-    )
-    value_gradient_matrix = (
-        token_value_matrix.reshape(token_rows, KEY_VALUE_HEADS, per_key_value_head, HEAD_FEATURES)
-        .sum(axis=2)
-        .reshape(token_rows, key_value_features)
-    )
+    values = gather_values(adapter_values, chips, reach)
+    info = jnp.concatenate(
+        [(lax.axis_index("seq") // 2).astype(jnp.int32)[None], packed_document_lengths[0]]
+    )
+    grad_queries, grad_pairs = attend(info, queries, grads, keys, values)
+    rotated_query_gradient, parts = give_back(grad_queries, grad_pairs, chips, reach)
+    summed = parts.astype(jnp.float32).sum(axis=0)
+    rotated_key_gradient = summed[0].astype(jnp.bfloat16)
+    value_gradient_matrix = summed[1]
     value_grad_low = value_gradient_matrix.astype(jnp.bfloat16)
     adapter_rank_gradient = ADAPTER_SCALE * lax.dot_general(
         value_gradient_matrix, up_widened, (((1,), (1,)), ((), ())), precision=lax.Precision.HIGHEST
     )
     reduced_rank_gradient = adapter_rank_gradient.astype(jnp.bfloat16)
-    frozen_path_gradient = contract_trailing(
-        value_grad_low, lax.all_gather(frozen_value_weight, "fsdp", axis=0, tiled=True)
-    )
-    input_gradient = (
-        frozen_path_gradient
-        + jnp.dot(reduced_rank_gradient, adapter_down_weight, preferred_element_type=jnp.float32)
-    ).astype(jnp.bfloat16)
     overall_token_count = token_rows * seq_count * fsdp_count
     down_shard = (
         lax.dot_general(
@@ -376,10 +803,15 @@
     adapter_down_gradient, adapter_up_gradient = sum_over_mesh(
         down_shard, up_shard, seq_count, fsdp_count
     )
+    frozen_path_gradient = contract_trailing(value_grad_low, weight)
+    input_gradient = (
+        frozen_path_gradient
+        + jnp.dot(reduced_rank_gradient, adapter_down_weight, preferred_element_type=jnp.float32)
+    ).astype(jnp.bfloat16)
     return (
-        input_gradient.reshape(1, token_rows, model_features),
-        rotated_query_gradient,
-        rotated_key_gradient,
+        input_gradient[None],
+        rotated_query_gradient[None],
+        rotated_key_gradient[None],
         adapter_down_gradient,
         adapter_up_gradient,
     )

time: 350 us -> 181 us (0.52); the launches traced: 346 us -> 180 us
  Pallas kernels: 51.2 us -> 156 us
  waiting for transfers between devices: 70.7 us -> 0 us
  matrix products: 73.3 us -> 15.4 us
  local copies, waits for them, and re-layouts: 63 us -> 5.49 us
  starting transfers between devices: 40.4 us -> 0 us
  other arithmetic: 30.6 us -> 3.18 us
  between operations: 16.3 us -> 0.78 us
    pallas_call x0 -> x4, Pallas kernels: none -> 123 us  [the longest x1 58.8 us: gather_all(): pl.pallas_call(functools.partial(gather_kernel, chips, depth, reach), out...]
    all_to_all x7 -> x0, waiting for transfers between devices: 70 us -> none  [the longest x1 22.7 us: body(): lax.all_to_all(grad_values, 'seq', split_axis=0, concat_axis=1, tiled=True)]
    dot_general x41 -> x1, matrix products: 63.1 us -> 4.67 us  [body(): jnp.dot(hidden_activations, weight, preferred_element_type=jnp.float32)]
    all_to_all x7 -> x0, starting transfers between devices: 40.4 us -> none  [the longest x1 8.58 us: body(): lax.all_to_all(attention_output_gradient.reshape(shaped), 'seq', split_ax...]
    slice x26 -> x1, local copies, waits for them, and re-layouts: 28.9 us -> 0.67 us  [body(): rotated_key_gradient = summed[0].astype(jnp.bfloat16)]
    unnamed x300 -> x12, local copies, waits for them, and re-layouts: 22.4 us -> 2.15 us
    pallas_call x1, Pallas kernels: 51.2 us -> 33 us  [sum_over_mesh(): pl.pallas_call(functools.partial(sum_kernel, chips, fsdp_count), out_shap...]
    convert_element_type x8 -> x0, other arithmetic: 9.47 us -> none  [body(): grad_scores = (probs_full * (grad_probs - row_delta)).astype(jnp.bfloat16)]
  transfers between devices with their start and end apart: 8 -> 0, of which waited for: 5 -> 0; matrix products, arithmetic and copies ran while one was open for 35% -> 0% of each run, Pallas kernels for 15% -> 0%
where the time goes in v2:
time: 181 us; the launch traced here: 180 us
  Pallas kernels  156 us (86%)
  matrix products  15.4 us (9%)
  local copies, waits for them, and re-layouts  5.49 us (3%)
  other arithmetic  3.18 us (2%)
    pallas_call x1, Pallas kernels, gather_all(): pl.pallas_call(functools.partial(gather_kernel, chips, depth, reach), out...  58.8 us
    pallas_call x1, Pallas kernels, sum_over_mesh(): pl.pallas_call(functools.partial(sum_kernel, chips, fsdp_count), out_shap...  33 us
    pallas_call x1, Pallas kernels, give_back(): pl.pallas_call(functools.partial(return_kernel, chips, reach), out_shape=...  24 us
    pallas_call x1, Pallas kernels, attend(): pl.pallas_call(attention_kernel, grid_spec=pltpu.PrefetchScalarGridSpec(n...  21.7 us
    pallas_call x1, Pallas kernels, gather_values(): pl.pallas_call(functools.partial(halo_kernel, chips, reach), out_shape=ja...  18 us
    dot_general x2, matrix products, contract_trailing(): lax.dot_general(left_rows, right_rows, (((1,), (1,)), ((), ())), preferre...  6.83 us
    dot_general x1, matrix products, body(): jnp.dot(hidden_activations, weight, preferred_element_type=jnp.float32)  4.67 us

profile of v2, /device:TPU:1, one launch (start us, length us, event | category | flops | bytes accessed | tf_op | source)
XLA Modules:
  0.0 180.4 jit_solution(8294867265554984307)
XLA Ops:
  0.6 0.0 copy-start
  0.6 0.0 copy-start.4
  0.7 58.8 %gather_inputs.1 = (bf16[256,2048]{1,0:T(8,128)(2,1)}, bf16[256,2048]{1,0:T(8,128)(2,1)}, bf16[1280,256]{1,0:T(8,128)(2,1)}, bf16[8192,512]{1,0:T(8,128)(2,1)}) custom-call(bf16[128,4096]{1,0:T(8,128)(2,1)} %bitcast.52, bf16[128,4096]{1,0:T(8,128)(2,1)} %bitcast.53, bf16[128,512]{1,0:T(8,128)(2,1)} %bitcast.56, bf16[1024,512]{1,0:T(8,128)(2,1)} %w_ref.1), custom_call_target="tpu_custom_call" | custom-call | tf_op jit(solution)/shard_map/gather_inputs/pallas_call | solution.py:434
  59.5 0.0 copy-done.4
  59.5 0.6 pad_add_fusion.info_ref
  60.1 0.0 copy-done
  60.1 4.7 %fusion.8 = f32[128,512]{1,0:T(8,128)S(1)} fusion(bf16[8192,512]{1,0:T(8,128)(2,1)} %get-tuple-element.16, bf16[1,128,8192]{2,1,0:T(8,128)(2,1)S(1)} %copy-done), kind=kOutput, calls=%fused_computation.12 | convolution fusion | flops 1073741824 | bytes 10747904 | tf_op jit(solution)/shard_map/dot_general | solution.py:772
  64.7 0.0 copy-done.1
  64.8 0.0 copy-start.3
  64.8 0.6 fusion.3
  65.4 0.1 copy-done.3
  65.5 1.0 fusion.11.v_ref
  66.5 18.0 %gather_values.1.v_ref = bf16[1280,256]{1,0:T(8,128)(2,1)} custom-call(bf16[128,512]{1,0:T(8,128)(2,1)} %fusion.11.v_ref), custom_call_target="tpu_custom_call" | custom-call | tf_op jit(solution)/shard_map/gather_values/pallas_call | solution.py:477
  84.5 21.7 %attention_backward.1 = (bf16[256,2048]{1,0:T(8,128)(2,1)}, bf16[2,1280,256]{2,1,0:T(8,128)(2,1)}) custom-call(s32[9]{0:T(128)} %pad_add_fusion.info_ref, bf16[256,2048]{1,0:T(8,128)(2,1)} %get-tuple-element.13.q_ref, bf16[256,2048]{1,0:T(8,128)(2,1)} %get-tuple-element.14.o_ref, bf16[1280,256]{1,0:T(8,128)(2,1)} %get-tuple-element.15.k_ref, ...), custom_call_target="tpu_custom_call" | custom-call | tf_op jit(solution)/shard_map/attention_backward/pallas_call | solution.py:625
  106.2 24.0 %return_gradients.1 = (bf16[128,4096]{1,0:T(8,128)(2,1)}, bf16[5,2,128,512]{3,2,1,0:T(8,128)(2,1)}) custom-call(bf16[256,2048]{1,0:T(8,128)(2,1)} %get-tuple-element.17.dq_ref, bf16[2,1280,256]{2,1,0:T(8,128)(2,1)} %get-tuple-element.18.dkv_ref), custom_call_target="tpu_custom_call" | custom-call | tf_op jit(solution)/shard_map/return_gradients/pallas_call | solution.py:720
  130.2 1.6 convert_reduce_fusion
  131.8 6.2 %fusion.14 = f32[128,8192]{1,0:T(8,128)S(1)} fusion(bf16[8192,512]{1,0:T(8,128)(2,1)} %get-tuple-element.16, f32[2,128,512]{2,1,0:T(8,128)S(1)} %convert_reduce_fusion), kind=kOutput, calls=%fused_computation.23 | convolution fusion | flops 1073741824 | bytes 12713984 | tf_op jit(solution)/shard_map/dot_general | solution.py:735
  138.0 0.2 fusion.12
  138.2 2.1 %fusion.1 = bf16[1,128,8192]{2,1,0:T(8,128)(2,1)} fusion(f32[128,8192]{1,0:T(8,128)S(1)} %fusion.14, bf16[128,16]{0,1:T(8,128)(2,1)S(1)} %fusion.12, bf16[16,8192]{1,0:T(8,128)(2,1)S(1)} %copy-done.1), kind=kOutput, calls=%fused_computation.2 | convolution fusion | flops 35651584 | bytes 6557696 | tf_op jit(solution)/shard_map/dot_general | solution.py:809
  140.3 0.7 slice.30
  141.0 0.2 convolution_multiply_fusion.2
  141.3 0.4 convolution_multiply_fusion
  141.7 0.1 copy.20
  141.7 0.1 pad.2.clone
  141.8 1.0 maximum_maximum_fusion.parts_ref
  142.9 33.0 %adapter_sum.1 = f32[16,2,24,256]{3,2,1,0:T(8,128)} custom-call(f32[16,2,24,256]{3,2,1,0:T(8,128)} %maximum_maximum_fusion.parts_ref), custom_call_target="tpu_custom_call" | custom-call | tf_op jit(solution)/shard_map/adapter_sum/pallas_call | solution.py:189
  175.9 1.1 slice_bitcast_fusion
  177.0 0.8 copy.18
  177.8 1.0 slice_reduce_fusion
  178.8 0.6 reshape_squeeze.3
  179.5 0.0 copy-done.2
  179.5 1.0 copy.22
  (4 shorter events, 0.1 us)
Async XLA Ops:
  0.6 59.4 %copy-start = (bf16[1,128,8192]{2,1,0:T(8,128)(2,1)S(1)}, bf16[1,128,8192]{2,1,0:T(8,128)(2,1)}, u32[]{:S(2)}) copy-start(bf16[1,128,8192]{2,1,0:T(8,128)(2,1)} %param.8) | copy-start | bytes 6291460
  0.6 58.8 %copy-start.4 = (s32[1,8]{1,0:T(1,128)S(1)}, s32[1,8]{1,0:T(1,128)}, u32[]{:S(2)}) copy-start(s32[1,8]{1,0:T(1,128)} %param.15) | copy-start | bytes 100
  60.1 4.7 %copy-start.1 = (bf16[16,8192]{1,0:T(8,128)(2,1)S(1)}, bf16[16,8192]{1,0:T(8,128)(2,1)}, u32[]{:S(2)}) copy-start(bf16[16,8192]{1,0:T(8,128)(2,1)} %param.13) | copy-start | bytes 786436
  64.8 0.7 copy-start.3
  142.8 36.6 %copy-start.2 = (bf16[128,4096]{1,0:T(8,128)(2,1)S(1)}, bf16[128,4096]{1,0:T(8,128)(2,1)}, u32[]{:S(2)}) copy-start(bf16[128,4096]{1,0:T(8,128)(2,1)} %get-tuple-element.20) | copy-start | bytes 3145732

commit v3 on v2

--- a/solution.py
+++ b/solution.py
@@ -18,20 +18,30 @@
 
 
 MESH = pl.DeviceIdType.MESH
-SUM_ROWS = 24
 SUM_LANES = 256
+SUM_WIDE = 384
 
 
 def sum_kernel(
     chips,
     depth,
+    down_ref,
+    up_ref,
+    grad_ref,
+    rank_ref,
+    map_ref,
+    weight_ref,
+    down_out,
+    up_out,
+    input_out,
     parts_ref,
-    out_ref,
     pair_in,
     pair_total,
     chip_in,
-    chip_total,
     depth_in,
+    final_ref,
+    weight_in,
+    weight_sems,
     pair_send,
     pair_recv,
     chip_send,
@@ -48,12 +58,23 @@
     chip = me // 2
     core = lax.rem(me, 2)
     partner = chip * 2 + 1 - core
+    tiles = weight_sems.shape[0]
+    tile = weight_ref.shape[0] // tiles
 
     def chip_peer(offset):
         return lax.rem(chip + offset, chips) * 2 + core
 
     def depth_peer(offset):
         return lax.rem(layer + offset, depth)
+
+    def weight_copy(index):
+        rows = pl.ds(pl.multiple_of(index * tile, tile), tile)
+        return pltpu.make_async_copy(
+            weight_ref.at[rows, :], weight_in.at[rows, :], weight_sems.at[index]
+        )
+
+    for index in range(tiles):
+        weight_copy(index).start()
 
     barrier = pltpu.get_barrier_semaphore()
     pl.semaphore_signal(barrier, inc=1, device_id={"seq": partner}, device_id_type=MESH)
@@ -65,6 +86,17 @@
         pl.semaphore_signal(
             barrier, inc=1, device_id={"fsdp": depth_peer(offset)}, device_id_type=MESH
         )
+
+    spare = up_ref.shape[1] // 128
+    parts_ref[:, :, :, SUM_LANES:] = jnp.zeros_like(parts_ref[:, :, :, SUM_LANES:])
+    for index in range(spare):
+        parts_ref[index // 2, index % 2, :, SUM_LANES:] = up_ref[
+            :, index * 128 : (index + 1) * 128
+        ]
+    for index in range(2 * chips):
+        parts_ref[index // 2, index % 2, :, :SUM_LANES] = down_ref[
+            :, index * SUM_LANES : (index + 1) * SUM_LANES
+        ]
     pl.semaphore_wait(barrier, chips + depth - 1)
 
     pair = pltpu.make_async_remote_copy(
@@ -79,7 +111,7 @@
     pair.wait()
 
     def add_pair(index, carry):
-        pair_total[index] = parts_ref[index, core] + pair_in[index]
+        pair_total[index] = (parts_ref[index, core] + pair_in[index]).astype(jnp.bfloat16)
         return carry
 
     lax.fori_loop(0, chips, add_pair, 0)
@@ -97,40 +129,63 @@
         )
         copy.start()
         copies.append(copy)
+
+    def project(index, carry):
+        weight_copy(index).wait()
+        lanes = pl.ds(pl.multiple_of(index * tile, tile), tile)
+        gradient = lax.dot_general(
+            grad_ref[...],
+            weight_in[lanes, :],
+            (((1,), (1,)), ((), ())),
+            preferred_element_type=jnp.float32,
+        ) + jnp.dot(rank_ref[...], map_ref[:, lanes], preferred_element_type=jnp.float32)
+        input_out[:, lanes] = gradient.astype(jnp.bfloat16)
+        return carry
+
+    lax.fori_loop(0, tiles, project, 0)
+
     for copy in copies:
         copy.wait()
-    total = pair_total[chip]
+    total = pair_total[chip].astype(jnp.float32)
     for offset in range(chips - 1):
-        total = total + chip_in[offset]
-    chip_total[0] = total
+        total = total + chip_in[offset].astype(jnp.float32)
+    depth_in[layer] = total.astype(jnp.bfloat16)
 
     copies = []
     for offset in range(1, depth):
-        copy = pltpu.make_async_remote_copy(
-            src_ref=chip_total.at[0],
-            dst_ref=depth_in.at[offset - 1],
+        copies.append(
+            pltpu.make_async_remote_copy(
+                src_ref=depth_in.at[layer],
+                dst_ref=depth_in.at[layer],
+                send_sem=depth_send.at[offset - 1],
+                recv_sem=depth_recv.at[offset - 1],
+                device_id={"fsdp": depth_peer(offset)},
+                device_id_type=MESH,
+            )
+        )
+    for copy in copies:
+        copy.start()
+    for offset, copy in enumerate(copies, 1):
+        source = lax.rem(layer + depth - offset, depth)
+        copy.wait_send()
+        pltpu.make_async_remote_copy(
+            src_ref=depth_in.at[source],
+            dst_ref=depth_in.at[source],
             send_sem=depth_send.at[offset - 1],
             recv_sem=depth_recv.at[offset - 1],
             device_id={"fsdp": depth_peer(offset)},
             device_id_type=MESH,
-        )
-        copy.start()
-        copies.append(copy)
-    for copy in copies:
-        copy.wait()
-    rows = [total]
-    for offset in range(depth - 1):
-        rows.append(depth_in[offset])
-    final = rows[0]
-    for row in rows[1:]:
-        final = final + row
-    out_ref[chip, core] = final
+        ).wait_recv()
+    final = depth_in[0].astype(jnp.float32)
+    for index in range(1, depth):
+        final = final + depth_in[index].astype(jnp.float32)
+    final_ref[chip, core] = final.astype(jnp.bfloat16)
 
     gives = []
     for offset in range(1, chips):
         copy = pltpu.make_async_remote_copy(
-            src_ref=out_ref.at[chip, core],
-            dst_ref=out_ref.at[chip, core],
+            src_ref=final_ref.at[chip, core],
+            dst_ref=final_ref.at[chip, core],
             send_sem=give_send.at[offset - 1],
             recv_sem=give_recv.at[offset - 1],
             device_id={"seq": chip_peer(offset)},
@@ -138,65 +193,75 @@
         )
         copy.start()
         gives.append(copy)
+
+    def hand_copy(offset, sender):
+        owner = lax.rem(chip + chips - offset, chips)
+        return pltpu.make_async_remote_copy(
+            src_ref=final_ref.at[owner, sender],
+            dst_ref=final_ref.at[owner, sender],
+            send_sem=hand_send.at[offset],
+            recv_sem=hand_recv.at[offset],
+            device_id={"seq": partner},
+            device_id_type=MESH,
+        )
+
     hands = []
     for offset in range(chips):
-        owner = lax.rem(chip + chips - offset, chips)
         if offset:
-            got = pltpu.make_async_remote_copy(
-                src_ref=out_ref.at[owner, core],
-                dst_ref=out_ref.at[owner, core],
+            owner = lax.rem(chip + chips - offset, chips)
+            pltpu.make_async_remote_copy(
+                src_ref=final_ref.at[owner, core],
+                dst_ref=final_ref.at[owner, core],
                 send_sem=give_send.at[offset - 1],
                 recv_sem=give_recv.at[offset - 1],
                 device_id={"seq": chip_peer(offset)},
                 device_id_type=MESH,
-            )
-            got.wait_recv()
-        hand = pltpu.make_async_remote_copy(
-            src_ref=out_ref.at[owner, core],
-            dst_ref=out_ref.at[owner, core],
-            send_sem=hand_send.at[offset],
-            recv_sem=hand_recv.at[offset],
-            device_id={"seq": partner},
-            device_id_type=MESH,
-        )
+            ).wait_recv()
+        hand = hand_copy(offset, core)
         hand.start()
         hands.append(hand)
     for copy in gives:
         copy.wait_send()
     for offset, hand in enumerate(hands):
-        owner = lax.rem(chip + chips - offset, chips)
         hand.wait_send()
-        pltpu.make_async_remote_copy(
-            src_ref=out_ref.at[owner, 1 - core],
-            dst_ref=out_ref.at[owner, 1 - core],
-            send_sem=hand_send.at[offset],
-            recv_sem=hand_recv.at[offset],
-            device_id={"seq": partner},
-            device_id_type=MESH,
-        ).wait_recv()
-
-
-def sum_over_mesh(down_shard, up_shard, seq_count, fsdp_count):
+        hand_copy(offset, 1 - core).wait_recv()
+    for index in range(2 * chips):
+        down_out[:, index * SUM_LANES : (index + 1) * SUM_LANES] = final_ref[
+            index // 2, index % 2, :, :SUM_LANES
+        ].astype(jnp.float32)
+    for index in range(spare):
+        up_out[:, index * 128 : (index + 1) * 128] = final_ref[
+            index // 2, index % 2, :, SUM_LANES:
+        ].astype(jnp.float32)
+
+
+def sum_over_mesh(
+    down_shard, up_shard, value_grad, rank_grad, down_weight, weight, seq_count, fsdp_count
+):
     chips = seq_count // 2
-    rank, width = down_shard.shape
-    blocks = down_shard.reshape(rank, seq_count, SUM_LANES).transpose(1, 0, 2)
-    ups = up_shard.reshape(seq_count, 1, SUM_LANES)
-    parts = jnp.concatenate(
-        [blocks, ups, jnp.zeros((seq_count, SUM_ROWS - rank - 1, SUM_LANES), jnp.float32)], axis=1
-    ).reshape(chips, 2, SUM_ROWS, SUM_LANES)
-    block = (SUM_ROWS, SUM_LANES)
+    rank = down_shard.shape[0]
+    block = (rank, SUM_WIDE)
+    tiles = 8
     sems = pltpu.SemaphoreType.DMA
-    summed = pl.pallas_call(
+    vmem = pl.BlockSpec(memory_space=pltpu.VMEM)
+    return pl.pallas_call(
         functools.partial(sum_kernel, chips, fsdp_count),
-        out_shape=jax.ShapeDtypeStruct(parts.shape, jnp.float32),
-        in_specs=[pl.BlockSpec(memory_space=pltpu.VMEM)],
-        out_specs=pl.BlockSpec(memory_space=pltpu.VMEM),
+        out_shape=(
+            jax.ShapeDtypeStruct(down_shard.shape, jnp.float32),
+            jax.ShapeDtypeStruct(up_shard.shape, jnp.float32),
+            jax.ShapeDtypeStruct((value_grad.shape[0], weight.shape[0]), jnp.bfloat16),
+        ),
+        in_specs=[vmem] * 5 + [pl.BlockSpec(memory_space=pl.ANY)],
+        out_specs=(vmem,) * 3,
         scratch_shapes=[
+            pltpu.VMEM((chips, 2) + block, jnp.float32),
             pltpu.VMEM((chips,) + block, jnp.float32),
-            pltpu.VMEM((chips,) + block, jnp.float32),
-            pltpu.VMEM((chips - 1,) + block, jnp.float32),
-            pltpu.VMEM((1,) + block, jnp.float32),
-            pltpu.VMEM((fsdp_count - 1,) + block, jnp.float32),
+            pltpu.VMEM((chips,) + block, jnp.bfloat16),
+            pltpu.VMEM((chips - 1,) + block, jnp.bfloat16),
+            pltpu.VMEM((fsdp_count,) + block, jnp.bfloat16),
+            pltpu.VMEM((chips, 2) + block, jnp.bfloat16),
+            pltpu.VMEM(weight.shape, jnp.bfloat16),
+            sems((tiles,)),
             sems,
             sems,
             sems((chips - 1,)),
@@ -210,61 +275,154 @@
         ],
         compiler_params=pltpu.CompilerParams(collective_id=0, has_side_effects=True),
         name="adapter_sum",
-    )(parts).reshape(seq_count, SUM_ROWS, SUM_LANES)
-    down = summed[:, :rank].transpose(1, 0, 2).reshape(rank, width)
-    up = summed[:, rank].reshape(up_shard.shape)
-    return down, up
-
-
-def halo_copies(source_ref, target_ref, send_sems, recv_sems, chips, reach):
-    me = lax.axis_index("seq")
-    chip = me // 2
-    core = lax.rem(me, 2)
-    rows, width = source_ref.shape
-    half = width // 2
-    own = None
-    remote = []
-    for behind in range(reach + 1):
-        for cross in range(2):
-            to_core = core if cross == 0 else 1 - core
-            lanes = pl.ds(pl.multiple_of(to_core * half, half), half)
-            slot = pl.multiple_of(((reach - behind) * 2 + core) * rows, rows)
-            source = source_ref.at[:, lanes]
-            target = target_ref.at[pl.ds(slot, rows), :]
-            index = behind * 2 + cross
-            if index == 0:
-                own = pltpu.make_async_copy(source, target, send_sems.at[0])
-            else:
-                remote.append(
-                    pltpu.make_async_remote_copy(
-                        src_ref=source,
-                        dst_ref=target,
-                        send_sem=send_sems.at[index],
-                        recv_sem=recv_sems.at[index],
-                        device_id={"seq": lax.rem(chip + behind, chips) * 2 + to_core},
-                        device_id_type=MESH,
-                    )
-                )
-    return own, remote
-
-
-def greet_halo(barrier, chips, reach, step):
-    me = lax.axis_index("seq")
-    chip = me // 2
-    core = lax.rem(me, 2)
-    for away in range(reach + 1):
-        for cross in range(2):
-            if away == 0 and cross == 0:
-                continue
-            to_core = core if cross == 0 else 1 - core
-            peer = lax.rem(chip + chips + step * away, chips) * 2 + to_core
+    )(down_shard, up_shard, value_grad, rank_grad, down_weight, weight)
+
+
+SIDE = 4
+
+
+class Place:
+    def __init__(self):
+        me = lax.axis_index("seq")
+        self.chip = me // 2
+        self.core = lax.rem(me, 2)
+        self.column = lax.rem(self.chip, SIDE)
+        self.row = self.chip // SIDE
+        self.partner = me + 1 - 2 * self.core
+
+    def along_x(self, offset):
+        column = lax.rem(self.column + offset + SIDE, SIDE)
+        return (self.row * SIDE + column) * 2 + self.core
+
+    def along_y(self, offset):
+        row = lax.rem(self.row + offset + SIDE, SIDE)
+        return (row * SIDE + self.column) * 2 + self.core
+
+    def greet(self, barrier):
+        peers = [self.partner] + [self.along_x(i) for i in range(1, SIDE)]
+        peers += [self.along_y(1), self.along_y(-1)]
+        for peer in peers:
             pl.semaphore_signal(barrier, inc=1, device_id={"seq": peer}, device_id_type=MESH)
+        return len(peers)
+
+
+class Halo:
+    LINKS = SIDE + 2
+
+    def __init__(self, place, source_ref, target_ref, send_sems, recv_sems, local_sem):
+        self.place = place
+        self.target_ref = target_ref
+        self.send_sems, self.recv_sems = send_sems, recv_sems
+        rows, width = source_ref.shape
+        half = width // 2
+        self.block = 2 * rows
+        core = place.core
+        first = SIDE * self.block + core * rows
+        here = target_ref.at[pl.ds(pl.multiple_of(first, rows), rows), :]
+        mine = pl.ds(pl.multiple_of(core * half, half), half)
+        theirs = pl.ds(pl.multiple_of((1 - core) * half, half), half)
+        self.own = pltpu.make_async_copy(source_ref.at[:, mine], here, local_sem)
+        self.pair = pltpu.make_async_remote_copy(
+            src_ref=source_ref.at[:, theirs],
+            dst_ref=here,
+            send_sem=send_sems.at[0],
+            recv_sem=recv_sems.at[0],
+            device_id={"seq": place.partner},
+            device_id_type=MESH,
+        )
+
+    def copy(self, index, source, target, peer):
+        first = source * self.block
+        return pltpu.make_async_remote_copy(
+            src_ref=self.target_ref.at[
+                pl.ds(pl.multiple_of(first, self.block), self.block), :
+            ],
+            dst_ref=self.target_ref.at[pl.ds(target * self.block, self.block), :],
+            send_sem=self.send_sems.at[index],
+            recv_sem=self.recv_sems.at[index],
+            device_id={"seq": peer},
+            device_id_type=MESH,
+        )
+
+    def start(self):
+        self.own.start()
+        self.pair.start()
+
+    def along_x(self, offset):
+        wraps = (self.place.column + offset) // SIDE
+        index = 2 if offset == 1 else 3
+        copy = self.copy(
+            index, SIDE * (1 - wraps), SIDE - offset, self.place.along_x(offset)
+        )
+        return wraps, copy
+
+    def spread(self):
+        place = self.place
+        self.own.wait()
+        self.pair.wait()
+        self.vertical = self.copy(1, SIDE, 0, place.along_y(1))
+        self.vertical.start()
+        self.sideways = [self.along_x(1), self.along_x(SIDE - 1)]
+        for wraps, copy in self.sideways:
+
+            @pl.when(wraps == 0)
+            def _():
+                copy.start()
+
+        self.vertical.wait_recv()
+        for wraps, copy in self.sideways:
+
+            @pl.when(wraps == 1)
+            def _():
+                copy.start()
+
+    def relay(self):
+        place = self.place
+        inner = (place.column == 1) | (place.column == 2)
+        self.sideways[0][1].wait_recv()
+        forward = self.copy(4, SIDE - 1, SIDE - 2, place.along_x(1))
+
+        @pl.when(inner)
+        def _():
+            forward.start()
+
+        self.sideways[1][1].wait_recv()
+        backward = self.copy(5, 1, SIDE - 2, place.along_x(-1))
+
+        @pl.when(inner)
+        def _():
+            backward.start()
+
+        self.relays = (inner, forward, backward)
+
+    def finish(self):
+        inner, forward, backward = self.relays
+        left = self.place.column < SIDE // 2
+
+        @pl.when(left)
+        def _():
+            backward.wait_recv()
+
+        @pl.when(jnp.logical_not(left))
+        def _():
+            forward.wait_recv()
+
+        @pl.when(inner)
+        def _():
+            forward.wait_send()
+            backward.wait_send()
+
+        self.vertical.wait_send()
+        for _, copy in self.sideways:
+            copy.wait_send()
+
+
+RING_ROWS = 256
+SLICE_ROWS = 48
 
 
 def gather_kernel(
-    chips,
     depth,
-    reach,
     q_ref,
     o_ref,
     k_ref,
@@ -282,97 +440,133 @@
     ring_recv,
     hand_send,
     hand_recv,
+    deep_send,
+    deep_recv,
+    plane_send,
+    plane_recv,
+    pass_send,
+    pass_recv,
 ):
-    me = lax.axis_index("seq")
+    place = Place()
+    core, partner = place.core, place.partner
     layer = lax.axis_index("fsdp")
-    core = lax.rem(me, 2)
-    partner = me + 1 - 2 * core
     up = lax.rem(layer + 1, depth)
     down = lax.rem(layer + depth - 1, depth)
 
     barrier = pltpu.get_barrier_semaphore()
-    greet_halo(barrier, chips, reach, -1)
+    count = place.greet(barrier)
     for peer in (up, down):
         pl.semaphore_signal(barrier, inc=1, device_id={"fsdp": peer}, device_id_type=MESH)
-    pl.semaphore_wait(barrier, 2 * reach + 3)
+    pl.semaphore_wait(barrier, count + 2)
 
     shard = w_ref.shape[0]
-    half = shard // 2
+    half = RING_ROWS // 2
     quarter = half // 2
     steps = depth // 2
-
-    def ring_rows(block, step, way):
-        first = block * shard + core * half
+    group = SIDE * SLICE_ROWS
+    position = (place.column, place.row)
+
+    def block_at(step, way):
+        return lax.rem(layer + depth + (step if way else -step), depth)
+
+    def remote(rows, source_rows, send, recv, peer, source_ref=None):
+        return pltpu.make_async_remote_copy(
+            src_ref=(wc_ref if source_ref is None else source_ref).at[source_rows, :],
+            dst_ref=wc_ref.at[rows, :],
+            send_sem=send,
+            recv_sem=recv,
+            device_id=peer,
+            device_id_type=MESH,
+        )
+
+    def ring_rows(block, step, way, owner):
+        first = block * shard + owner * half
         if step < steps:
             return pl.ds(pl.multiple_of(first, half), half)
         return pl.ds(pl.multiple_of(first + way * quarter, quarter), quarter)
 
+    def slice_rows(block, axis, owner, spot):
+        first = block * shard + RING_ROWS + axis * 2 * group + owner * group + spot * SLICE_ROWS
+        return pl.ds(pl.multiple_of(first, 16), SLICE_ROWS)
+
+    def group_rows(block, axis, owner):
+        first = block * shard + RING_ROWS + axis * 2 * group + owner * group
+        return pl.ds(pl.multiple_of(first, 16), group)
+
     def ring_copy(step, way):
-        if way == 0:
-            block, peer = lax.rem(layer + depth - (step - 1), depth), up
+        rows = ring_rows(block_at(step - 1, way), step, way, core)
+        peer = {"fsdp": down if way else up}
+        sems = ring_send.at[way, step - 1], ring_recv.at[way, step - 1]
+        if step == 1:
+            source = ring_rows(0, step, way, core)
+            return remote(rows, source, *sems, peer, w_ref)
+        return remote(rows, rows, *sems, peer)
+
+    def ring_got(step, way):
+        rows = ring_rows(block_at(step, way), step, way, core)
+        sems = ring_send.at[way, step - 1], ring_recv.at[way, step - 1]
+        return remote(rows, rows, *sems, {"fsdp": up})
+
+    def ring_hand(step, way, owner):
+        rows = ring_rows(block_at(step, way), step, way, owner)
+        sems = hand_send.at[way, step - 1], hand_recv.at[way, step - 1]
+        return remote(rows, rows, *sems, {"seq": partner})
+
+    def deep_copy(step, way, axis):
+        rows = slice_rows(block_at(step - 1, way), axis, core, position[axis])
+        peer = {"fsdp": down if way else up}
+        sems = deep_send.at[way, step - 1, axis], deep_recv.at[way, step - 1, axis]
+        if step == 1:
+            source = slice_rows(0, axis, core, position[axis])
+            return remote(rows, source, *sems, peer, w_ref)
+        return remote(rows, rows, *sems, peer)
+
+    def deep_got(step, way, axis):
+        rows = slice_rows(block_at(step, way), axis, core, position[axis])
+        sems = deep_send.at[way, step - 1, axis], deep_recv.at[way, step - 1, axis]
+        return remote(rows, rows, *sems, {"fsdp": up})
+
+    def toward(axis, offset):
+        return {"seq": place.along_y(offset) if axis else place.along_x(offset)}
+
+    def plane_copy(number, block, axis, kind, sending):
+        step_forward = 1 if kind == 0 or (kind == 2 and number % 2) else -1
+        if kind == 2:
+            spot = -1 if step_forward == 1 else 1
+            if not sending:
+                spot = 2
         else:
-            block, peer = lax.rem(layer + (step - 1), depth), down
-        rows = ring_rows(block, step, way)
-        if step == 1:
-            first = core * half
-            source = w_ref.at[pl.ds(pl.multiple_of(first, half), half), :]
-            rows = pl.ds(pl.multiple_of(block * shard + first, half), half)
-        else:
-            source = wc_ref.at[rows, :]
-        return pltpu.make_async_remote_copy(
-            src_ref=source,
-            dst_ref=wc_ref.at[rows, :],
-            send_sem=ring_send.at[way, step - 1],
-            recv_sem=ring_recv.at[way, step - 1],
-            device_id={"fsdp": peer},
-            device_id_type=MESH,
-        )
-
-    def hand_copy(step, way, sender):
-        block = lax.rem(layer + depth + (step if way else -step), depth)
-        first = block * shard + sender * half
-        if step < steps:
-            rows = pl.ds(pl.multiple_of(first, half), half)
-        else:
-            rows = pl.ds(pl.multiple_of(first + way * quarter, quarter), quarter)
-        return pltpu.make_async_remote_copy(
-            src_ref=wc_ref.at[rows, :],
-            dst_ref=wc_ref.at[rows, :],
-            send_sem=hand_send.at[way, step - 1],
-            recv_sem=hand_recv.at[way, step - 1],
-            device_id={"seq": partner},
-            device_id_type=MESH,
-        )
-
-    def got_copy(step, way):
-        block = lax.rem(layer + depth + (step if way else -step), depth)
-        rows = ring_rows(block, step, way)
-        return pltpu.make_async_remote_copy(
-            src_ref=wc_ref.at[rows, :],
-            dst_ref=wc_ref.at[rows, :],
-            send_sem=ring_send.at[way, step - 1],
-            recv_sem=ring_recv.at[way, step - 1],
-            device_id={"fsdp": up},
-            device_id_type=MESH,
-        )
+            spot = 0 if sending else -step_forward
+        spot = lax.rem(position[axis] + spot + SIDE, SIDE)
+        rows = slice_rows(block, axis, core, spot)
+        sems = plane_send.at[axis, number - 1, kind], plane_recv.at[axis, number - 1, kind]
+        return remote(rows, rows, *sems, toward(axis, step_forward))
+
+    def pass_copy(number, block, axis, owner):
+        rows = group_rows(block, axis, owner)
+        sems = pass_send.at[axis, number - 1], pass_recv.at[axis, number - 1]
+        return remote(rows, rows, *sems, {"seq": partner})
 
     sent = []
-    for way in range(2):
-        copy = ring_copy(1, way)
+
+    def go(copy):
         copy.start()
         sent.append(copy)
 
-    own_key, keys = halo_copies(k_ref, kc_ref, halo_send, halo_recv, chips, reach)
-    for copy in keys:
-        copy.start()
-    own_key.start()
+    halo = Halo(place, k_ref, kc_ref, halo_send, halo_recv, local_sem.at[3])
+    halo.start()
+    for way in range(2):
+        for axis in range(2):
+            go(deep_copy(1, way, axis))
+    for way in range(2):
+        go(ring_copy(1, way))
     rows = q_ref.shape[0]
     wide = q_ref.shape[1] // 2
     here = pl.ds(pl.multiple_of(core * rows, rows), rows)
     mine = pl.ds(pl.multiple_of(core * wide, wide), wide)
     theirs = pl.ds(pl.multiple_of((1 - core) * wide, wide), wide)
     pairs = []
-    locals_ = [own_key]
+    locals_ = []
     for index, (source_ref, target_ref) in enumerate(((q_ref, qc_ref), (o_ref, oc_ref))):
         copy = pltpu.make_async_remote_copy(
             src_ref=source_ref.at[:, theirs],
@@ -396,93 +590,147 @@
     )
     copy.start()
     locals_.append(copy)
-
-    hands = []
-    for step in range(1, steps + 1):
+    halo.spread()
+
+    numbers = 2 * steps - 1
+    blocks = {}
+    for number in range(1, numbers + 1):
+        step, way = (number + 1) // 2, (number - 1) % 2
+        blocks[number] = block_at(step, way)
+
+    def pass_on(number):
+        for axis in range(2):
+            plane_copy(number, blocks[number], axis, 0 if number % 2 else 1, False).wait_recv()
+            go(plane_copy(number, blocks[number], axis, 2, True))
+
+    def hand_over(number):
+        for axis in range(2):
+            plane_copy(number, blocks[number], axis, 1 if number % 2 else 0, False).wait_recv()
+            plane_copy(number, blocks[number], axis, 2, False).wait_recv()
+            go(pass_copy(number, blocks[number], axis, core))
+
+    def ring_step(step):
         for way in range(2):
-            got_copy(step, way).wait_recv()
+            ring_got(step, way).wait_recv()
             if step < steps:
-                copy = ring_copy(step + 1, way)
-                copy.start()
-                sent.append(copy)
-            copy = hand_copy(step, way, core)
-            copy.start()
-            hands.append(copy)
+                go(ring_copy(step + 1, way))
+            go(ring_hand(step, way, core))
+
+    for number in range(1, numbers + 1):
+        step, way = (number + 1) // 2, (number - 1) % 2
+        for axis in range(2):
+            came = axis if step == steps else way
+            deep_got(step, came, axis).wait_recv()
+            if step + 1 < steps or (step + 1 == steps and axis == way):
+                go(deep_copy(step + 1, way, axis))
+            for kind in range(2):
+                go(plane_copy(number, blocks[number], axis, kind, True))
+        if number == 1:
+            halo.relay()
+        if number > 1:
+            pass_on(number - 1)
+        if number > 2:
+            hand_over(number - 2)
+        if number % 2 == 0:
+            ring_step(number // 2)
+    pass_on(numbers)
+    hand_over(numbers - 1)
+    ring_step(steps)
+    hand_over(numbers)
+
+    halo.finish()
     for copy in locals_:
+        copy.wait()
+    for copy in pairs:
         copy.wait()
     for copy in sent:
         copy.wait_send()
-    for copy in hands:
-        copy.wait_send()
+    for number in range(1, numbers + 1):
+        for axis in range(2):
+            pass_copy(number, blocks[number], axis, 1 - core).wait_recv()
     for step in range(1, steps + 1):
         for way in range(2):
-            hand_copy(step, way, 1 - core).wait_recv()
-    for copy in keys:
-        copy.wait()
-    for copy in pairs:
-        copy.wait()
-
-
-def gather_all(queries, grads, keys, weight, chips, depth, reach):
+            ring_hand(step, way, 1 - core).wait_recv()
+
+
+def gather_all(queries, grads, keys, weight, depth):
     rows, width = queries.shape
     kv = keys.shape[1]
     sems = pltpu.SemaphoreType.DMA
-    links = 2 * (reach + 1)
+    steps = depth // 2
+    numbers = 2 * steps - 1
     anywhere = pl.BlockSpec(memory_space=pl.ANY)
     vmem = pl.BlockSpec(memory_space=pltpu.VMEM)
     dtype = jnp.bfloat16
     return pl.pallas_call(
-        functools.partial(gather_kernel, chips, depth, reach),
+        functools.partial(gather_kernel, depth),
         out_shape=(
             jax.ShapeDtypeStruct((2 * rows, width // 2), dtype),
             jax.ShapeDtypeStruct((2 * rows, width // 2), dtype),
-            jax.ShapeDtypeStruct((links * rows, kv // 2), dtype),
+            jax.ShapeDtypeStruct(((SIDE + 1) * 2 * rows, kv // 2), dtype),
             jax.ShapeDtypeStruct((depth * weight.shape[0], weight.shape[1]), dtype),
         ),
         in_specs=[vmem] * 4,
         out_specs=(anywhere,) * 4,
         scratch_shapes=[
-            sems((links,)),
-            sems((links,)),
+            sems((Halo.LINKS,)),
+            sems((Halo.LINKS,)),
             sems((2,)),
             sems((2,)),
-            sems((3,)),
-            sems((2, depth // 2)),
-            sems((2, depth // 2)),
-            sems((2, depth // 2)),
-            sems((2, depth // 2)),
+            sems((4,)),
+            sems((2, steps)),
+            sems((2, steps)),
+            sems((2, steps)),
+            sems((2, steps)),
+            sems((2, steps, 2)),
+            sems((2, steps, 2)),
+            sems((2, numbers, 3)),
+            sems((2, numbers, 3)),
+            sems((2, numbers)),
+            sems((2, numbers)),
         ],
         compiler_params=pltpu.CompilerParams(collective_id=1, has_side_effects=True),
         name="gather_inputs",
     )(queries, grads, keys, weight)
 
 
-def halo_kernel(chips, reach, v_ref, vc_ref, send_sems, recv_sems):
+def halo_kernel(v_ref, vc_ref, send_sems, recv_sems, local_sem):
+    place = Place()
     barrier = pltpu.get_barrier_semaphore()
-    greet_halo(barrier, chips, reach, -1)
-    pl.semaphore_wait(barrier, 2 * reach + 1)
-    own, remote = halo_copies(v_ref, vc_ref, send_sems, recv_sems, chips, reach)
-    for copy in remote:
-        copy.start()
-    own.start()
-    own.wait()
-    for copy in remote:
-        copy.wait()
-
-
-def gather_values(values, chips, reach):
+    count = place.greet(barrier)
+    pl.semaphore_wait(barrier, count)
+    halo = Halo(place, v_ref, vc_ref, send_sems, recv_sems, local_sem)
+    halo.start()
+    halo.spread()
+    halo.relay()
+    halo.finish()
+
+
+def gather_values(values):
     rows, kv = values.shape
-    links = 2 * (reach + 1)
     sems = pltpu.SemaphoreType.DMA
     return pl.pallas_call(
-        functools.partial(halo_kernel, chips, reach),
-        out_shape=jax.ShapeDtypeStruct((links * rows, kv // 2), values.dtype),
+        halo_kernel,
+        out_shape=jax.ShapeDtypeStruct(((SIDE + 1) * 2 * rows, kv // 2), values.dtype),
         in_specs=[pl.BlockSpec(memory_space=pltpu.VMEM)],
         out_specs=pl.BlockSpec(memory_space=pl.ANY),
-        scratch_shapes=[sems((links,)), sems((links,))],
+        scratch_shapes=[sems((Halo.LINKS,)), sems((Halo.LINKS,)), sems],
         compiler_params=pltpu.CompilerParams(collective_id=2, has_side_effects=True),
         name="gather_values",
     )(values)
+
+
+def greet_halo(barrier, chips, reach, step):
+    me = lax.axis_index("seq")
+    chip = me // 2
+    core = lax.rem(me, 2)
+    for away in range(reach + 1):
+        for cross in range(2):
+            if away == 0 and cross == 0:
+                continue
+            to_core = core if cross == 0 else 1 - core
+            peer = lax.rem(chip + chips + step * away, chips) * 2 + to_core
+            pl.semaphore_signal(barrier, inc=1, device_id={"seq": peer}, device_id_type=MESH)
 
 
 def attention_kernel(
@@ -761,9 +1009,7 @@
         attention_output_gradient[0],
         stored_rotated_keys[0],
         frozen_value_weight,
-        chips,
         fsdp_count,
-        reach,
     )
     adapter_projection = contract_trailing(hidden_activations, adapter_down_weight)
     adapter_maps = ADAPTER_SCALE * jnp.dot(
@@ -771,7 +1017,7 @@
     )
     base_value = jnp.dot(hidden_activations, weight, preferred_element_type=jnp.float32)
     adapter_values = (base_value + adapter_maps).astype(jnp.bfloat16)
-    values = gather_values(adapter_values, chips, reach)
+    values = gather_values(adapter_values)
     info = jnp.concatenate(
         [(lax.axis_index("seq") // 2).astype(jnp.int32)[None], packed_document_lengths[0]]
     )
@@ -800,14 +1046,16 @@
         * jnp.dot(adapter_projection.T, value_gradient_matrix, precision=lax.Precision.HIGHEST)
         / overall_token_count
     )
-    adapter_down_gradient, adapter_up_gradient = sum_over_mesh(
-        down_shard, up_shard, seq_count, fsdp_count
-    )
-    frozen_path_gradient = contract_trailing(value_grad_low, weight)
-    input_gradient = (
-        frozen_path_gradient
-        + jnp.dot(reduced_rank_gradient, adapter_down_weight, preferred_element_type=jnp.float32)
-    ).astype(jnp.bfloat16)
+    adapter_down_gradient, adapter_up_gradient, input_gradient = sum_over_mesh(
+        down_shard,
+        up_shard,
+        value_grad_low,
+        reduced_rank_gradient,
+        adapter_down_weight,
+        weight,
+        seq_count,
+        fsdp_count,
+    )
     return (
         input_gradient[None],
         rotated_query_gradient[None],

time: 181 us -> 165 us (0.912)
  Pallas kernels: 156 us -> 145 us
  matrix products: 15.4 us -> 9.54 us
    pallas_call x2, Pallas kernels: 76.8 us -> 66.9 us  [the longest x1 50.1 us: gather_all(): pl.pallas_call(functools.partial(gather_kernel, depth), out_shape=(jax.Sh...]
    dot_general x2 -> x1, matrix products: 6.83 us -> 1.59 us  [contract_trailing(): lax.dot_general(left_rows, right_rows, (((1,), (1,)), ((), ())), preferre...]
    unnamed x12 -> x16, local copies, waits for them, and re-layouts: 2.15 us -> 6.19 us
    pallas_call x1, Pallas kernels: 33 us -> 30.7 us  [sum_over_mesh(): pl.pallas_call(functools.partial(sum_kernel, chips, fsdp_count), out_shap...]
    dot_general x1 -> x0, matrix products: 2.12 us -> none  [body(): jnp.dot(reduced_rank_gradient, adapter_down_weight, preferred_element_typ...]
    pallas_call x1, Pallas kernels: 24 us -> 25.9 us  [give_back(): pl.pallas_call(functools.partial(return_kernel, chips, reach), out_shape=...]
where the time goes in v3:
time: 165 us
  Pallas kernels  145 us (88%)
  matrix products  9.54 us (6%)
  local copies, waits for them, and re-layouts  6.93 us (4%)
  other arithmetic  2.94 us (2%)
    pallas_call x1, Pallas kernels, gather_all(): pl.pallas_call(functools.partial(gather_kernel, depth), out_shape=(jax.Sh...  50.1 us
    pallas_call x1, Pallas kernels, sum_over_mesh(): pl.pallas_call(functools.partial(sum_kernel, chips, fsdp_count), out_shap...  30.7 us
    pallas_call x1, Pallas kernels, give_back(): pl.pallas_call(functools.partial(return_kernel, chips, reach), out_shape=...  25.9 us
    pallas_call x1, Pallas kernels, attend(): pl.pallas_call(attention_kernel, grid_spec=pltpu.PrefetchScalarGridSpec(n...  21.5 us
    pallas_call x1, Pallas kernels, gather_values(): pl.pallas_call(halo_kernel, out_shape=jax.ShapeDtypeStruct(((SIDE + 1) *...  16.8 us
    unnamed x16, local copies, waits for them, and re-layouts  6.19 us
    dot_general x1, matrix products, body(): jnp.dot(hidden_activations, weight, preferred_element_type=jnp.float32)  4.64 us

profile of v3, /device:TPU:1, one launch (start us, length us, event | category | flops | bytes accessed | tf_op | source)
XLA Modules:
  0.0 165.1 jit_solution(10258865748012599164)
XLA Ops:
  0.6 0.0 copy-start
  0.7 1.4 pad_add_fusion.info_ref
  2.0 0.2 copy-done
  2.2 1.6 fusion.1
  3.8 50.1 %gather_inputs.1 = (bf16[256,2048]{1,0:T(8,128)(2,1)}, bf16[256,2048]{1,0:T(8,128)(2,1)}, bf16[1280,256]{1,0:T(8,128)(2,1)}, bf16[8192,512]{1,0:T(8,128)(2,1)}) custom-call(bf16[128,4096]{1,0:T(8,128)(2,1)} %bitcast.32, bf16[128,4096]{1,0:T(8,128)(2,1)} %bitcast.33, bf16[128,512]{1,0:T(8,128)(2,1)} %bitcast.35, bf16[1024,512]{1,0:T(8,128)(2,1)} %w_ref.1), custom_call_target="tpu_custom_call" | custom-call | tf_op jit(solution)/shard_map/gather_inputs/pallas_call | solution.py:665
  53.9 0.0 copy-start.4
  53.9 4.6 %fusion.6 = f32[128,512]{1,0:T(8,128)S(1)} fusion(bf16[8192,512]{1,0:T(8,128)(2,1)} %get-tuple-element.19.weight_ref, bf16[1,128,8192]{2,1,0:T(8,128)(2,1)S(1)} %copy-done), kind=kOutput, calls=%fused_computation.9 | convolution fusion | flops 1073741824 | bytes 10747904 | tf_op jit(solution)/shard_map/dot_general | solution.py:1018
  58.6 0.0 copy-done.4
  58.6 1.0 fusion.9.v_ref
  59.6 16.8 %gather_values.1.v_ref = bf16[1280,256]{1,0:T(8,128)(2,1)} custom-call(bf16[128,512]{1,0:T(8,128)(2,1)} %fusion.9.v_ref), custom_call_target="tpu_custom_call" | custom-call | tf_op jit(solution)/shard_map/gather_values/pallas_call | solution.py:712
  76.4 21.5 %attention_backward.1 = (bf16[256,2048]{1,0:T(8,128)(2,1)}, bf16[2,1280,256]{2,1,0:T(8,128)(2,1)}) custom-call(s32[9]{0:T(128)} %pad_add_fusion.info_ref, bf16[256,2048]{1,0:T(8,128)(2,1)} %get-tuple-element.16.q_ref, bf16[256,2048]{1,0:T(8,128)(2,1)} %get-tuple-element.17.o_ref, bf16[1280,256]{1,0:T(8,128)(2,1)} %get-tuple-element.18.k_ref, ...), custom_call_target="tpu_custom_call" | custom-call | tf_op jit(solution)/shard_map/attention_backward/pallas_call | solution.py:873
  97.9 25.9 %return_gradients.1 = (bf16[128,4096]{1,0:T(8,128)(2,1)}, bf16[5,2,128,512]{3,2,1,0:T(8,128)(2,1)}) custom-call(bf16[256,2048]{1,0:T(8,128)(2,1)} %get-tuple-element.20.dq_ref, bf16[2,1280,256]{2,1,0:T(8,128)(2,1)} %get-tuple-element.21.dkv_ref), custom_call_target="tpu_custom_call" | custom-call | tf_op jit(solution)/shard_map/return_gradients/pallas_call | solution.py:968
  123.8 1.6 convert_reduce_fusion
  125.3 0.9 convolution_multiply_fusion.3.up_ref
  126.2 0.3 fusion.10.rank_ref
  126.4 0.0 copy-start.3
  126.5 0.7 fusion.12
  127.2 1.2 convolution_multiply_fusion.down_ref
  128.4 0.0 copy-done.3
  128.4 30.7 %adapter_sum.1 = (f32[16,8192]{1,0:T(8,128)}, f32[16,512]{1,0:T(8,128)}, bf16[128,8192]{1,0:T(8,128)(2,1)}) custom-call(f32[16,8192]{1,0:T(8,128)} %convolution_multiply_fusion.down_ref, f32[16,512]{1,0:T(8,128)} %convolution_multiply_fusion.3.up_ref, bf16[128,512]{1,0:T(8,128)(2,1)} %get-tuple-element.28.grad_ref, bf16[128,16]{1,0:T(8,128)(2,1)} %copy-done.3, ...), custom_call_target="tpu_custom_call" | custom-call | tf_op jit(solution)/shard_map/adapter_sum/pallas_call | solution.py:247
  159.1 0.0 copy-start.1
  159.1 3.2 %copy.21 = bf16[1,128,8192]{2,1,0:T(8,128)(2,1)} copy(bf16[1,128,8192]{2,1,0:T(8,128)(2,1)} %bitcast.31) | data formatting | bytes 4194304
  162.3 0.0 copy-done.1
  162.3 0.0 copy-start.2
  162.3 0.0 copy-start.5
  162.3 1.0 copy.22
  163.3 0.4 copy-done.2
  163.7 0.8 copy.23
  164.5 0.0 copy-done.5
  164.5 0.6 copy.24
Async XLA Ops:
  0.6 1.6 copy-start
  53.9 4.7 %copy-start.4 = (bf16[16,512]{1,0:T(8,128)(2,1)S(1)}, bf16[16,512]{1,0:T(8,128)(2,1)}, u32[]{:S(2)}) copy-start(bf16[16,512]{1,0:T(8,128)(2,1)} %param.14) | copy-start | bytes 49156
  126.4 2.0 %copy-start.3 = (bf16[128,16]{1,0:T(8,128)(2,1)}, bf16[128,16]{1,0:T(8,128)(2,1)S(1)}, u32[]{:S(2)}) copy-start(bf16[128,16]{1,0:T(8,128)(2,1)S(1)} %fusion.10.rank_ref) | copy-start | bytes 12292
  159.1 3.2 %copy-start.1 = (bf16[128,4096]{1,0:T(8,128)(2,1)S(1)}, bf16[128,4096]{1,0:T(8,128)(2,1)}, u32[]{:S(2)}) copy-start(bf16[128,4096]{1,0:T(8,128)(2,1)} %get-tuple-element.24) | copy-start | bytes 3145732
  162.3 1.4 copy-start.2
  162.3 2.2 %copy-start.5 = (f32[16,512]{1,0:T(8,128)S(1)}, f32[16,512]{1,0:T(8,128)}, u32[]{:S(2)}) copy-start(f32[16,512]{1,0:T(8,128)} %get-tuple-element.38) | copy-start | bytes 98308

commit v4 on v3

--- a/solution.py
+++ b/solution.py
@@ -417,29 +417,29 @@
             copy.wait_send()
 
 
-RING_ROWS = 256
-SLICE_ROWS = 48
-
-
 def gather_kernel(
     depth,
     q_ref,
     o_ref,
     k_ref,
     w_ref,
+    x_ref,
+    map_ref,
+    up_ref,
     qc_ref,
     oc_ref,
     kc_ref,
     wc_ref,
+    low_ref,
+    v_ref,
+    weight,
+    total,
     halo_send,
     halo_recv,
     pair_send,
     pair_recv,
     local_sem,
-    ring_send,
-    ring_recv,
-    hand_send,
-    hand_recv,
+    store_sem,
     deep_send,
     deep_recv,
     plane_send,
@@ -460,10 +460,10 @@
     pl.semaphore_wait(barrier, count + 2)
 
     shard = w_ref.shape[0]
-    half = RING_ROWS // 2
-    quarter = half // 2
+    group = shard // 4
+    part = group // SIDE
     steps = depth // 2
-    group = SIDE * SLICE_ROWS
+    numbers = 2 * steps - 1
     position = (place.column, place.row)
 
     def block_at(step, way):
@@ -471,46 +471,21 @@
 
     def remote(rows, source_rows, send, recv, peer, source_ref=None):
         return pltpu.make_async_remote_copy(
-            src_ref=(wc_ref if source_ref is None else source_ref).at[source_rows, :],
-            dst_ref=wc_ref.at[rows, :],
+            src_ref=(weight if source_ref is None else source_ref).at[source_rows, :],
+            dst_ref=weight.at[rows, :],
             send_sem=send,
             recv_sem=recv,
             device_id=peer,
             device_id_type=MESH,
         )
 
-    def ring_rows(block, step, way, owner):
-        first = block * shard + owner * half
-        if step < steps:
-            return pl.ds(pl.multiple_of(first, half), half)
-        return pl.ds(pl.multiple_of(first + way * quarter, quarter), quarter)
-
     def slice_rows(block, axis, owner, spot):
-        first = block * shard + RING_ROWS + axis * 2 * group + owner * group + spot * SLICE_ROWS
-        return pl.ds(pl.multiple_of(first, 16), SLICE_ROWS)
+        first = block * shard + axis * 2 * group + owner * group + spot * part
+        return pl.ds(pl.multiple_of(first, part), part)
 
     def group_rows(block, axis, owner):
-        first = block * shard + RING_ROWS + axis * 2 * group + owner * group
-        return pl.ds(pl.multiple_of(first, 16), group)
-
-    def ring_copy(step, way):
-        rows = ring_rows(block_at(step - 1, way), step, way, core)
-        peer = {"fsdp": down if way else up}
-        sems = ring_send.at[way, step - 1], ring_recv.at[way, step - 1]
-        if step == 1:
-            source = ring_rows(0, step, way, core)
-            return remote(rows, source, *sems, peer, w_ref)
-        return remote(rows, rows, *sems, peer)
-
-    def ring_got(step, way):
-        rows = ring_rows(block_at(step, way), step, way, core)
-        sems = ring_send.at[way, step - 1], ring_recv.at[way, step - 1]
-        return remote(rows, rows, *sems, {"fsdp": up})
-
-    def ring_hand(step, way, owner):
-        rows = ring_rows(block_at(step, way), step, way, owner)
-        sems = hand_send.at[way, step - 1], hand_recv.at[way, step - 1]
-        return remote(rows, rows, *sems, {"seq": partner})
+        first = block * shard + axis * 2 * group + owner * group
+        return pl.ds(pl.multiple_of(first, group), group)
 
     def deep_copy(step, way, axis):
         rows = slice_rows(block_at(step - 1, way), axis, core, position[axis])
@@ -532,9 +507,7 @@
     def plane_copy(number, block, axis, kind, sending):
         step_forward = 1 if kind == 0 or (kind == 2 and number % 2) else -1
         if kind == 2:
-            spot = -1 if step_forward == 1 else 1
-            if not sending:
-                spot = 2
+            spot = -step_forward if sending else 2
         else:
             spot = 0 if sending else -step_forward
         spot = lax.rem(position[axis] + spot + SIDE, SIDE)
@@ -553,13 +526,11 @@
         copy.start()
         sent.append(copy)
 
-    halo = Halo(place, k_ref, kc_ref, halo_send, halo_recv, local_sem.at[3])
+    for axis in range(2):
+        for way in range(2):
+            go(deep_copy(1, way, axis))
+    halo = Halo(place, k_ref, kc_ref, halo_send, halo_recv, local_sem.at[2])
     halo.start()
-    for way in range(2):
-        for axis in range(2):
-            go(deep_copy(1, way, axis))
-    for way in range(2):
-        go(ring_copy(1, way))
     rows = q_ref.shape[0]
     wide = q_ref.shape[1] // 2
     here = pl.ds(pl.multiple_of(core * rows, rows), rows)
@@ -583,60 +554,86 @@
         )
         copy.start()
         locals_.append(copy)
-    copy = pltpu.make_async_copy(
-        w_ref,
-        wc_ref.at[pl.ds(pl.multiple_of(layer * shard, shard), shard), :],
-        local_sem.at[2],
-    )
-    copy.start()
-    locals_.append(copy)
+
+    def store(index, source, block):
+        target = wc_ref.at[pl.ds(pl.multiple_of(block * shard, shard), shard), :]
+        copy = pltpu.make_async_copy(source, target, store_sem.at[index])
+        copy.start()
+        locals_.append(copy)
+
+    def project(block, rows_of_weight):
+        lanes = pl.ds(pl.multiple_of(block * shard, shard), shard)
+        return jnp.dot(x_ref[:, lanes], rows_of_weight, preferred_element_type=jnp.float32)
+
+    store(0, w_ref, layer)
     halo.spread()
-
-    numbers = 2 * steps - 1
+    low = lax.dot_general(
+        x_ref[...],
+        map_ref[...],
+        (((1,), (1,)), ((), ())),
+        preferred_element_type=jnp.float32,
+    )
+    low_ref[...] = low
+    total[...] = project(layer, w_ref[...]) + ADAPTER_SCALE * jnp.dot(
+        low,
+        up_ref[...].astype(jnp.float32),
+        precision=lax.Precision.HIGHEST,
+        preferred_element_type=jnp.float32,
+    )
+
     blocks = {}
+    members = {}
     for number in range(1, numbers + 1):
         step, way = (number + 1) // 2, (number - 1) % 2
         blocks[number] = block_at(step, way)
-
-    def pass_on(number):
-        for axis in range(2):
-            plane_copy(number, blocks[number], axis, 0 if number % 2 else 1, False).wait_recv()
-            go(plane_copy(number, blocks[number], axis, 2, True))
-
-    def hand_over(number):
-        for axis in range(2):
-            plane_copy(number, blocks[number], axis, 1 if number % 2 else 0, False).wait_recv()
-            plane_copy(number, blocks[number], axis, 2, False).wait_recv()
-            go(pass_copy(number, blocks[number], axis, core))
-
-    def ring_step(step):
-        for way in range(2):
-            ring_got(step, way).wait_recv()
-            if step < steps:
-                go(ring_copy(step + 1, way))
-            go(ring_hand(step, way, core))
-
-    for number in range(1, numbers + 1):
-        step, way = (number + 1) // 2, (number - 1) % 2
-        for axis in range(2):
-            came = axis if step == steps else way
-            deep_got(step, came, axis).wait_recv()
-            if step + 1 < steps or (step + 1 == steps and axis == way):
-                go(deep_copy(step + 1, way, axis))
-            for kind in range(2):
-                go(plane_copy(number, blocks[number], axis, kind, True))
-        if number == 1:
+        members.setdefault(step, []).append(number)
+
+    def pass_on(step):
+        for number in members.get(step, ()):
+            for axis in range(2):
+                kind = 0 if number % 2 else 1
+                plane_copy(number, blocks[number], axis, kind, False).wait_recv()
+                go(plane_copy(number, blocks[number], axis, 2, True))
+
+    def hand_over(step):
+        for number in members.get(step, ()):
+            for axis in range(2):
+                kind = 1 if number % 2 else 0
+                plane_copy(number, blocks[number], axis, kind, False).wait_recv()
+                plane_copy(number, blocks[number], axis, 2, False).wait_recv()
+                go(pass_copy(number, blocks[number], axis, core))
+
+    def use(step):
+        for number in members.get(step, ()):
+            block = blocks[number]
+            for axis in range(2):
+                pass_copy(number, block, axis, 1 - core).wait_recv()
+            first = pl.ds(pl.multiple_of(block * shard, shard), shard)
+            store(number, weight.at[first, :], block)
+            total[...] += project(block, weight[first, :])
+
+    for step in range(1, steps + 1):
+        for number in members[step]:
+            way = (number - 1) % 2
+            for axis in range(2):
+                came = axis if step == steps else way
+                deep_got(step, came, axis).wait_recv()
+                if step + 1 < steps or (step + 1 == steps and axis == way):
+                    go(deep_copy(step + 1, way, axis))
+                for kind in range(2):
+                    go(plane_copy(number, blocks[number], axis, kind, True))
+        pass_on(step - 1)
+        if step == 2:
             halo.relay()
-        if number > 1:
-            pass_on(number - 1)
-        if number > 2:
-            hand_over(number - 2)
-        if number % 2 == 0:
-            ring_step(number // 2)
-    pass_on(numbers)
-    hand_over(numbers - 1)
-    ring_step(steps)
-    hand_over(numbers)
+        hand_over(step - 2)
+        use(step - 3)
+    hand_over(steps - 1)
+    pass_on(steps)
+    use(steps - 2)
+    use(steps - 1)
+    hand_over(steps)
+    use(steps)
+    v_ref[...] = total[...].astype(jnp.bfloat16)
 
     halo.finish()
     for copy in locals_:
@@ -645,15 +642,9 @@
         copy.wait()
     for copy in sent:
         copy.wait_send()
-    for number in range(1, numbers + 1):
-        for axis in range(2):
-            pass_copy(number, blocks[number], axis, 1 - core).wait_recv()
-    for step in range(1, steps + 1):
-        for way in range(2):
-            ring_hand(step, way, 1 - core).wait_recv()
-
-
-def gather_all(queries, grads, keys, weight, depth):
+
+
+def gather_all(queries, grads, keys, weight, hidden, down_weight, up_weight, depth):
     rows, width = queries.shape
     kv = keys.shape[1]
     sems = pltpu.SemaphoreType.DMA
@@ -662,26 +653,28 @@
     anywhere = pl.BlockSpec(memory_space=pl.ANY)
     vmem = pl.BlockSpec(memory_space=pltpu.VMEM)
     dtype = jnp.bfloat16
+    whole = (depth * weight.shape[0], weight.shape[1])
     return pl.pallas_call(
         functools.partial(gather_kernel, depth),
         out_shape=(
             jax.ShapeDtypeStruct((2 * rows, width // 2), dtype),
             jax.ShapeDtypeStruct((2 * rows, width // 2), dtype),
             jax.ShapeDtypeStruct(((SIDE + 1) * 2 * rows, kv // 2), dtype),
-            jax.ShapeDtypeStruct((depth * weight.shape[0], weight.shape[1]), dtype),
+            jax.ShapeDtypeStruct(whole, dtype),
+            jax.ShapeDtypeStruct((rows, down_weight.shape[0]), jnp.float32),
+            jax.ShapeDtypeStruct((rows, kv), dtype),
         ),
-        in_specs=[vmem] * 4,
-        out_specs=(anywhere,) * 4,
+        in_specs=[vmem] * 7,
+        out_specs=(anywhere,) * 4 + (vmem,) * 2,
         scratch_shapes=[
+            pltpu.VMEM(whole, dtype),
+            pltpu.VMEM((rows, kv), jnp.float32),
             sems((Halo.LINKS,)),
             sems((Halo.LINKS,)),
             sems((2,)),
             sems((2,)),
-            sems((4,)),
-            sems((2, steps)),
-            sems((2, steps)),
-            sems((2, steps)),
-            sems((2, steps)),
+            sems((3,)),
+            sems((numbers + 1,)),
             sems((2, steps, 2)),
             sems((2, steps, 2)),
             sems((2, numbers, 3)),
@@ -691,67 +684,69 @@
         ],
         compiler_params=pltpu.CompilerParams(collective_id=1, has_side_effects=True),
         name="gather_inputs",
-    )(queries, grads, keys, weight)
-
-
-def halo_kernel(v_ref, vc_ref, send_sems, recv_sems, local_sem):
-    place = Place()
-    barrier = pltpu.get_barrier_semaphore()
-    count = place.greet(barrier)
-    pl.semaphore_wait(barrier, count)
-    halo = Halo(place, v_ref, vc_ref, send_sems, recv_sems, local_sem)
-    halo.start()
-    halo.spread()
-    halo.relay()
-    halo.finish()
-
-
-def gather_values(values):
-    rows, kv = values.shape
-    sems = pltpu.SemaphoreType.DMA
-    return pl.pallas_call(
-        halo_kernel,
-        out_shape=jax.ShapeDtypeStruct(((SIDE + 1) * 2 * rows, kv // 2), values.dtype),
-        in_specs=[pl.BlockSpec(memory_space=pltpu.VMEM)],
-        out_specs=pl.BlockSpec(memory_space=pl.ANY),
-        scratch_shapes=[sems((Halo.LINKS,)), sems((Halo.LINKS,)), sems],
-        compiler_params=pltpu.CompilerParams(collective_id=2, has_side_effects=True),
-        name="gather_values",
-    )(values)
-
-
-def greet_halo(barrier, chips, reach, step):
-    me = lax.axis_index("seq")
-    chip = me // 2
-    core = lax.rem(me, 2)
-    for away in range(reach + 1):
-        for cross in range(2):
-            if away == 0 and cross == 0:
-                continue
-            to_core = core if cross == 0 else 1 - core
-            peer = lax.rem(chip + chips + step * away, chips) * 2 + to_core
+    )(queries, grads, keys, weight, hidden, down_weight, up_weight)
+
+
+class Window:
+    def __init__(self, chips):
+        self.chips = chips
+        me = lax.axis_index("seq")
+        self.chip = me // 2
+        self.core = lax.rem(me, 2)
+        self.partner = me + 1 - 2 * self.core
+
+    def peer(self, away, cross):
+        chip = lax.rem(self.chip + self.chips + away, self.chips)
+        return chip * 2 + (1 - self.core if cross else self.core)
+
+    def links(self):
+        return [(away, cross) for away in range(SIDE, -1, -1) for cross in range(2)][:-2] + [(0, 1)]
+
+    def greet(self, barrier):
+        peers = [self.peer(away, cross) for away, cross in self.links()]
+        peers += [self.peer(-away, cross) for away, cross in self.links() if away]
+        for peer in peers:
             pl.semaphore_signal(barrier, inc=1, device_id={"seq": peer}, device_id_type=MESH)
+        pl.semaphore_wait(barrier, len(peers))
 
 
 def attention_kernel(
+    chips,
     info_ref,
     q_ref,
     o_ref,
     k_ref,
     v_ref,
     dq_ref,
-    dkv_ref,
+    dk_ref,
+    dv_ref,
     bias_ref,
     s_ref,
     g_ref,
     p_ref,
     d_ref,
     acc_ref,
+    values_ref,
+    give_ref,
+    back_ref,
+    query_ref,
+    came_ref,
+    value_send,
+    value_recv,
+    back_send,
+    back_recv,
+    query_send,
+    query_recv,
 ):
+    net = Window(chips)
+    core = net.core
     chip = info_ref[0]
+    group = pl.program_id(0)
     side = pl.program_id(1)
+    groups = 2
     rows = q_ref.shape[0]
-    heads = q_ref.shape[1] // HEAD_FEATURES
+    wide = q_ref.shape[1]
+    heads = wide // HEAD_FEATURES
     window = bias_ref.shape[0]
     span = k_ref.shape[0]
     start = pl.multiple_of(side * rows, rows)
@@ -760,9 +755,66 @@
     chunk = 128
     count = window // chunk
 
+    def kv_lanes(owner, head):
+        first = (owner * groups + head) * HEAD_FEATURES
+        return pl.ds(pl.multiple_of(first, HEAD_FEATURES), HEAD_FEATURES)
+
+    def slot(away, owner):
+        return pl.ds(pl.multiple_of(((SIDE - away) * 2 + owner) * rows, rows), rows)
+
+    def value_copy(head, away, cross):
+        to_core = 1 - core if cross else core
+        index = away * 2 + cross
+        return pltpu.make_async_remote_copy(
+            src_ref=v_ref.at[:, kv_lanes(to_core, head)],
+            dst_ref=values_ref.at[head, slot(away, core), :],
+            send_sem=value_send.at[head, index],
+            recv_sem=value_recv.at[head, index],
+            device_id={"seq": net.peer(away, cross)},
+            device_id_type=MESH,
+        )
+
+    def back_copy(head, away, cross):
+        to_core = 1 - core if cross else core
+        index = away * 2 + cross
+        return pltpu.make_async_remote_copy(
+            src_ref=give_ref.at[head, :, slot(away, to_core), :],
+            dst_ref=back_ref.at[away, :, :, kv_lanes(core, head)],
+            send_sem=back_send.at[head, index],
+            recv_sem=back_recv.at[head, index],
+            device_id={"seq": net.peer(-away, cross)},
+            device_id_type=MESH,
+        )
+
+    def query_copy(head):
+        return pltpu.make_async_remote_copy(
+            src_ref=query_ref.at[head, 1 - core],
+            dst_ref=came_ref.at[head],
+            send_sem=query_send.at[head],
+            recv_sem=query_recv.at[head],
+            device_id={"seq": net.partner},
+            device_id_type=MESH,
+        )
+
+    @pl.when((group == 0) & (side == 0))
+    def _():
+        net.greet(pltpu.get_barrier_semaphore())
+        for head in range(groups):
+            for link in net.links():
+                value_copy(head, *link).start()
+        for head in range(groups):
+            values_ref[head, slot(0, core), :] = v_ref[:, kv_lanes(core, head)]
+
     @pl.when(side == 0)
     def _():
         acc_ref[...] = jnp.zeros_like(acc_ref)
+
+    for head in range(groups):
+
+        @pl.when((group == head) & (side == 0))
+        def _():
+            for link in net.links():
+                value_copy(head, *link).wait_recv()
 
     q_place = chip * (2 * rows) + start + lax.broadcasted_iota(jnp.int32, (1, rows), 1)
     finish = jnp.int32(0)
@@ -819,7 +871,7 @@
             here = slice(part * chunk, (part + 1) * chunk)
             weights = jnp.exp2((s_ref[here, :] - peak) * steep)
             grad_probs = lax.dot_general(
-                v_ref[pl.ds(start + part * chunk, chunk), :],
+                values_ref[group, pl.ds(start + part * chunk, chunk), :],
                 o_pair,
                 trailing,
                 preferred_element_type=jnp.float32,
@@ -843,6 +895,16 @@
     acc_ref[1, rows_here, :] += jnp.dot(
         p_ref[...], stack(o_ref, 0, heads), preferred_element_type=jnp.float32
     )
+
+    for head in range(groups):
+
+        @pl.when((group == head) & (side == 1))
+        def _():
+            give_ref[head] = acc_ref[...].astype(jnp.bfloat16)
+            for link in net.links():
+                back_copy(head, *link).start()
+            back_ref[0, :, :, kv_lanes(core, head)] = give_ref[head, :, slot(0, core), :]
+
     grad_t = lax.dot_general(
         k_ref[rows_here, :],
         d_ref[...],
@@ -851,16 +913,38 @@
     )
     for head in range(heads):
         block = grad_t[:, head * rows : (head + 1) * rows]
-        dq_ref[:, head * HEAD_FEATURES : (head + 1) * HEAD_FEATURES] = (
+        query_ref[group, side, :, head * HEAD_FEATURES : (head + 1) * HEAD_FEATURES] = (
             block.T * inverse
         ).astype(jnp.bfloat16)
 
-    @pl.when(side == 1)
+    for head in range(groups):
+
+        @pl.when((group == head) & (side == 1))
+        def _():
+            query_copy(head).start()
+
+    @pl.when((group == groups - 1) & (side == 1))
     def _():
-        dkv_ref[...] = acc_ref[...].astype(jnp.bfloat16)
-
-
-def attend(info, queries, grads, keys, values):
+        for head in range(groups):
+            here = pl.ds(pl.multiple_of((core * groups + head) * wide, wide), wide)
+            there = pl.ds(pl.multiple_of(((1 - core) * groups + head) * wide, wide), wide)
+            query_copy(head).wait()
+            dq_ref[:, here] = query_ref[head, core]
+            dq_ref[:, there] = came_ref[head]
+        for head in range(groups):
+            for link in net.links():
+                back_copy(head, *link).wait()
+                value_copy(head, *link).wait_send()
+        grad_k = back_ref[0, 0].astype(jnp.float32)
+        grad_v = back_ref[0, 1].astype(jnp.float32)
+        for away in range(1, SIDE + 1):
+            grad_k = grad_k + back_ref[away, 0].astype(jnp.float32)
+            grad_v = grad_v + back_ref[away, 1].astype(jnp.float32)
+        dk_ref[...] = grad_k.astype(jnp.bfloat16)
+        dv_ref[...] = grad_v
+
+
+def attend(info, queries, grads, keys, values, chips):
     tokens, width = queries.shape
     rows = tokens // 2
     span, kv = keys.shape
@@ -868,20 +952,21 @@
     wide = width // groups
     window = span - rows
     stacked = rows * wide // HEAD_FEATURES
+    links = 2 * (SIDE + 1)
+    sems = pltpu.SemaphoreType.DMA
     query_spec = pl.BlockSpec((rows, wide), lambda group, side, info_ref: (side, group))
     key_spec = pl.BlockSpec((span, HEAD_FEATURES), lambda group, side, info_ref: (0, group))
+
+    def still(shape):
+        return pl.BlockSpec(shape, lambda group, side, info_ref: (0, 0))
+
     return pl.pallas_call(
-        attention_kernel,
+        functools.partial(attention_kernel, chips),
         grid_spec=pltpu.PrefetchScalarGridSpec(
             num_scalar_prefetch=1,
             grid=(groups, 2),
-            in_specs=[query_spec, query_spec, key_spec, key_spec],
-            out_specs=(
-                query_spec,
-                pl.BlockSpec(
-                    (2, span, HEAD_FEATURES), lambda group, side, info_ref: (0, 0, group)
-                ),
-            ),
+            in_specs=[query_spec, query_spec, key_spec, still(values.shape)],
+            out_specs=(still((rows, 2 * width)), still(values.shape), still(values.shape)),
             scratch_shapes=[
                 pltpu.VMEM((window, rows), jnp.float32),
                 pltpu.VMEM((window, 2 * rows), jnp.float32),
@@ -889,94 +974,27 @@
                 pltpu.VMEM((window, stacked), jnp.bfloat16),
                 pltpu.VMEM((window, stacked), jnp.bfloat16),
                 pltpu.VMEM((2, span, HEAD_FEATURES), jnp.float32),
+                pltpu.VMEM((groups, span, HEAD_FEATURES), jnp.bfloat16),
+                pltpu.VMEM((groups, 2, span, HEAD_FEATURES), jnp.bfloat16),
+                pltpu.VMEM((SIDE + 1, 2) + values.shape, jnp.bfloat16),
+                pltpu.VMEM((groups, 2, rows, wide), jnp.bfloat16),
+                pltpu.VMEM((groups, rows, wide), jnp.bfloat16),
+                sems((groups, links)),
+                sems((groups, links)),
+                sems((groups, links)),
+                sems((groups, links)),
+                sems((groups,)),
+                sems((groups,)),
             ],
         ),
         out_shape=(
-            jax.ShapeDtypeStruct((tokens, width), jnp.bfloat16),
-            jax.ShapeDtypeStruct((2, span, kv), jnp.bfloat16),
+            jax.ShapeDtypeStruct((rows, 2 * width), jnp.bfloat16),
+            jax.ShapeDtypeStruct(values.shape, jnp.bfloat16),
+            jax.ShapeDtypeStruct(values.shape, jnp.float32),
         ),
+        compiler_params=pltpu.CompilerParams(collective_id=3, has_side_effects=True),
         name="attention_backward",
     )(info, queries, grads, keys, values)
-
-
-def return_kernel(
-    chips, reach, dq_ref, dkv_ref, full_ref, parts_ref, send_sems, recv_sems, pair_send, pair_recv, local_sem
-):
-    me = lax.axis_index("seq")
-    chip = me // 2
-    core = lax.rem(me, 2)
-    partner = me + 1 - 2 * core
-    barrier = pltpu.get_barrier_semaphore()
-    greet_halo(barrier, chips, reach, 1)
-    pl.semaphore_wait(barrier, 2 * reach + 1)
-
-    rows = full_ref.shape[0]
-    wide = dq_ref.shape[1]
-    half = dkv_ref.shape[2]
-    kv_lanes = pl.ds(pl.multiple_of(core * half, half), half)
-    waits = []
-    for behind in range(reach, -1, -1):
-        for cross in range(2):
-            to_core = core if cross == 0 else 1 - core
-            slot = pl.multiple_of(((reach - behind) * 2 + to_core) * rows, rows)
-            source = dkv_ref.at[:, pl.ds(slot, rows), :]
-            target = parts_ref.at[behind, :, :, kv_lanes]
-            index = behind * 2 + cross
-            if index == 0:
-                copy = pltpu.make_async_copy(source, target, local_sem.at[0])
-            else:
-                copy = pltpu.make_async_remote_copy(
-                    src_ref=source,
-                    dst_ref=target,
-                    send_sem=send_sems.at[index],
-                    recv_sem=recv_sems.at[index],
-                    device_id={"seq": lax.rem(chip + chips - behind, chips) * 2 + to_core},
-                    device_id_type=MESH,
-                )
-            copy.start()
-            waits.append(copy)
-    lanes = pl.ds(pl.multiple_of(core * wide, wide), wide)
-    copy = pltpu.make_async_remote_copy(
-        src_ref=dq_ref.at[pl.ds(pl.multiple_of((1 - core) * rows, rows), rows), :],
-        dst_ref=full_ref.at[:, lanes],
-        send_sem=pair_send,
-        recv_sem=pair_recv,
-        device_id={"seq": partner},
-        device_id_type=MESH,
-    )
-    copy.start()
-    waits.append(copy)
-    copy = pltpu.make_async_copy(
-        dq_ref.at[pl.ds(pl.multiple_of(core * rows, rows), rows), :],
-        full_ref.at[:, lanes],
-        local_sem.at[1],
-    )
-    copy.start()
-    waits.append(copy)
-    for copy in waits:
-        copy.wait()
-
-
-def give_back(grad_queries, grad_pairs, chips, reach):
-    tokens, width = grad_queries.shape
-    kv = grad_pairs.shape[2]
-    rows = tokens // 2
-    links = 2 * (reach + 1)
-    sems = pltpu.SemaphoreType.DMA
-    anywhere = pl.BlockSpec(memory_space=pl.ANY)
-    vmem = pl.BlockSpec(memory_space=pltpu.VMEM)
-    return pl.pallas_call(
-        functools.partial(return_kernel, chips, reach),
-        out_shape=(
-            jax.ShapeDtypeStruct((rows, 2 * width), jnp.bfloat16),
-            jax.ShapeDtypeStruct((reach + 1, 2, rows, 2 * kv), jnp.bfloat16),
-        ),
-        in_specs=[vmem, vmem],
-        out_specs=(anywhere, anywhere),
-        scratch_shapes=[sems((links,)), sems((links,)), sems, sems, sems((2,))],
-        compiler_params=pltpu.CompilerParams(collective_id=3, has_side_effects=True),
-        name="return_gradients",
-    )(grad_queries, grad_pairs)
 
 
 def contract_trailing(left_rows, right_rows):
@@ -1001,31 +1019,24 @@
     seq_count = lax.axis_size("seq")
     fsdp_count = lax.axis_size("fsdp")
     chips = seq_count // 2
-    reach = DOC_MOST // (2 * token_rows)
     up_widened = adapter_up_weight.astype(jnp.float32)
 
-    queries, grads, keys, weight = gather_all(
+    queries, grads, keys, weight, adapter_projection, adapter_values = gather_all(
         stored_rotated_queries[0],
         attention_output_gradient[0],
         stored_rotated_keys[0],
         frozen_value_weight,
+        hidden_activations,
+        adapter_down_weight,
+        adapter_up_weight,
         fsdp_count,
     )
-    adapter_projection = contract_trailing(hidden_activations, adapter_down_weight)
-    adapter_maps = ADAPTER_SCALE * jnp.dot(
-        adapter_projection, up_widened, precision=lax.Precision.HIGHEST
-    )
-    base_value = jnp.dot(hidden_activations, weight, preferred_element_type=jnp.float32)
-    adapter_values = (base_value + adapter_maps).astype(jnp.bfloat16)
-    values = gather_values(adapter_values)
     info = jnp.concatenate(
         [(lax.axis_index("seq") // 2).astype(jnp.int32)[None], packed_document_lengths[0]]
     )
-    grad_queries, grad_pairs = attend(info, queries, grads, keys, values)
-    rotated_query_gradient, parts = give_back(grad_queries, grad_pairs, chips, reach)
-    summed = parts.astype(jnp.float32).sum(axis=0)
-    rotated_key_gradient = summed[0].astype(jnp.bfloat16)
-    value_gradient_matrix = summed[1]
+    rotated_query_gradient, rotated_key_gradient, value_gradient_matrix = attend(
+        info, queries, grads, keys, adapter_values, chips
+    )
     value_grad_low = value_gradient_matrix.astype(jnp.bfloat16)
     adapter_rank_gradient = ADAPTER_SCALE * lax.dot_general(
         value_gradient_matrix, up_widened, (((1,), (1,)), ((), ())), precision=lax.Precision.HIGHEST

time: 165 us -> 140 us (0.85)
  Pallas kernels: 145 us -> 125 us
  matrix products: 9.54 us -> 4.27 us
    pallas_call x3 -> x1, Pallas kernels: 64.2 us -> 45.5 us  [attend(): pl.pallas_call(functools.partial(attention_kernel, chips), grid_spec=pltp...]
    dot_general x3 -> x0, matrix products: 7.2 us -> none  [the longest x1 4.64 us: body(): jnp.dot(hidden_activations, weight, preferred_element_type=jnp.float32)]
    unnamed x16 -> x21, local copies, waits for them, and re-layouts: 6.19 us -> 6.27 us
where the time goes in v4:
time: 140 us; the launch traced here: 139 us
  Pallas kernels  125 us (89%)
  local copies, waits for them, and re-layouts  6.27 us (4%)
  matrix products  4.27 us (3%)
  other arithmetic  2.88 us (2%)
    pallas_call x1, Pallas kernels, gather_all(): pl.pallas_call(functools.partial(gather_kernel, depth), out_shape=(jax.Sh...  50.5 us
    pallas_call x1, Pallas kernels, attend(): pl.pallas_call(functools.partial(attention_kernel, chips), grid_spec=pltp...  45.5 us
    pallas_call x1, Pallas kernels, sum_over_mesh(): pl.pallas_call(functools.partial(sum_kernel, chips, fsdp_count), out_shap...  29.2 us
    unnamed x21, local copies, waits for them, and re-layouts  6.27 us

profile of v4, /device:TPU:1, one launch (start us, length us, event | category | flops | bytes accessed | tf_op | source)
XLA Modules:
  0.0 139.3 jit_solution(1695299754557056045)
XLA Ops:
  0.6 1.2 pad_add_fusion.info_ref
  1.9 50.5 %gather_inputs.1 = (bf16[256,2048]{1,0:T(8,128)(2,1)}, bf16[256,2048]{1,0:T(8,128)(2,1)}, bf16[1280,256]{1,0:T(8,128)(2,1)}, bf16[8192,512]{1,0:T(8,128)(2,1)}, ...) custom-call(bf16[128,4096]{1,0:T(8,128)(2,1)} %bitcast.19, bf16[128,4096]{1,0:T(8,128)(2,1)} %bitcast.20, ...), custom_call_target="tpu_custom_call" | custom-call | tf_op jit(solution)/shard_map/gather_inputs/pallas_call | solution.py:657
  52.4 0.0 copy-start.6
  52.4 0.0 copy-start.5
  52.4 0.0 copy-start
  52.4 45.5 %attention_backward.1 = (bf16[128,4096]{1,0:T(8,128)(2,1)}, bf16[128,512]{1,0:T(8,128)(2,1)}, f32[128,512]{1,0:T(8,128)}) custom-call(s32[9]{0:T(128)} %pad_add_fusion.info_ref, bf16[256,2048]{1,0:T(8,128)(2,1)} %get-tuple-element.17.q_ref, bf16[256,2048]{1,0:T(8,128)(2,1)} %get-tuple-element.18.o_ref, bf16[1280,256]{1,0:T(8,128)(2,1)} %get-tuple-element.19.k_ref, ...), custom_call_target="tpu_custom_call" | custom-call | tf_op jit(solution)/shard_map/attention_backward/pallas_call | solution.py:963
  97.9 0.0 copy-done.6
  97.9 1.8 %convolution_multiply_fusion.2.up_ref = f32[16,512]{1,0:T(8,128)} fusion(f32[128,16]{1,0:T(8,128)S(1)} %copy-done.6, f32[128,512]{1,0:T(8,128)} %get-tuple-element.21), kind=kOutput, calls=%fused_computation.3 | convolution fusion | flops 12591104 | bytes 303104 | tf_op jit(solution)/shard_map/dot_general | solution.py:1057
  99.8 0.0 copy-done.5
  99.8 1.2 fusion.rank_ref
  101.0 0.0 copy-start.3
  101.0 1.6 %convert_element_type.8.grad_ref = bf16[128,512]{1,0:T(8,128)(2,1)} convert(f32[128,512]{1,0:T(8,128)} %get-tuple-element.21) | non-fusion elementwise | flops 65536 | bytes 393216 | tf_op jit(solution)/shard_map/convert_element_type | solution.py:1040
  102.6 0.0 copy-done
  102.6 1.2 convolution_multiply_fusion.down_ref
  103.8 0.0 copy-done.3
  103.9 29.2 %adapter_sum.1 = (f32[16,8192]{1,0:T(8,128)}, f32[16,512]{1,0:T(8,128)}, bf16[128,8192]{1,0:T(8,128)(2,1)}) custom-call(f32[16,8192]{1,0:T(8,128)} %convolution_multiply_fusion.down_ref, f32[16,512]{1,0:T(8,128)} %convolution_multiply_fusion.2.up_ref, bf16[128,512]{1,0:T(8,128)(2,1)} %convert_element_type.8.grad_ref, bf16[128,16]{1,0:T(8,128)(2,1)} %copy-done.3, ...), custom_call_target="tpu_custom_call" | custom-call | tf_op jit(solution)/shard_map/adapter_sum/pallas_call | solution.py:247
  133.1 0.0 copy-start.1
  133.1 3.2 %copy.20 = bf16[1,128,8192]{2,1,0:T(8,128)(2,1)} copy(bf16[1,128,8192]{2,1,0:T(8,128)(2,1)} %bitcast.17) | data formatting | bytes 4194304
  136.2 0.0 copy-done.1
  136.2 0.0 copy-start.4
  136.2 0.0 copy-start.2
  136.3 0.0 copy-start.7
  136.3 1.0 copy.21
  137.2 0.0 copy-done.4
  137.2 0.7 copy.22
  137.9 0.0 copy-done.2
  137.9 0.8 copy.23
  138.7 0.0 copy-done.7
  138.7 0.6 copy.24
Async XLA Ops:
  52.4 45.6 %copy-start.6 = (f32[128,16]{1,0:T(8,128)S(1)}, f32[128,16]{1,0:T(8,128)}, u32[]{:S(2)}) copy-start(f32[128,16]{1,0:T(8,128)} %get-tuple-element.22) | copy-start | bytes 24580
  52.4 47.4 %copy-start.5 = (bf16[16,512]{1,0:T(8,128)(2,1)S(1)}, bf16[16,512]{1,0:T(8,128)(2,1)}, u32[]{:S(2)}) copy-start(bf16[16,512]{1,0:T(8,128)(2,1)} %up_ref.1) | copy-start | bytes 49156
  52.4 50.3 %copy-start = (bf16[1,128,8192]{2,1,0:T(8,128)(2,1)S(1)}, bf16[1,128,8192]{2,1,0:T(8,128)(2,1)}, u32[]{:S(2)}) copy-start(bf16[1,128,8192]{2,1,0:T(8,128)(2,1)} %param.8) | copy-start | bytes 6291460
  101.0 2.9 %copy-start.3 = (bf16[128,16]{1,0:T(8,128)(2,1)}, bf16[128,16]{1,0:T(8,128)(2,1)S(1)}, u32[]{:S(2)}) copy-start(bf16[128,16]{1,0:T(8,128)(2,1)S(1)} %fusion.rank_ref) | copy-start | bytes 12292
  133.1 3.2 %copy-start.1 = (bf16[128,4096]{1,0:T(8,128)(2,1)S(1)}, bf16[128,4096]{1,0:T(8,128)(2,1)}, u32[]{:S(2)}) copy-start(bf16[128,4096]{1,0:T(8,128)(2,1)} %get-tuple-element.25) | copy-start | bytes 3145732
  136.2 1.0 copy-start.4
  136.2 1.7 %copy-start.2 = (f32[16,8192]{1,0:T(8,128)S(1)}, f32[16,8192]{1,0:T(8,128)}, u32[]{:S(2)}) copy-start(f32[16,8192]{1,0:T(8,128)} %get-tuple-element.37) | copy-start | bytes 1572868
  136.3 2.4 %copy-start.7 = (f32[16,512]{1,0:T(8,128)S(1)}, f32[16,512]{1,0:T(8,128)}, u32[]{:S(2)}) copy-start(f32[16,512]{1,0:T(8,128)} %get-tuple-element.38) | copy-start | bytes 98308
